TPU v7x, 128 devices: a whole 4x4x4 slice. The times are simulated.
128 devices in a mesh: req: 16 (over y, x), tp: 8 (over z, core).
Axes of the slice: x: 4, y: 4, z: 4, core: 2. Of those that a mesh axis runs over, the one named last changes fastest.
Arguments:
- stream: bfloat16 [512, 2048], P('req'), may hold values from -1.5 to 1.5
- attn_gain: bfloat16 [2048], replicated, may hold values from 0.25 to 1.75
- mlp_gain: bfloat16 [2048], replicated, may hold values from 0.25 to 1.75
- w_query: bfloat16 [2048, 2048], P(None, 'tp'), may hold values from -0.125 to 0.125
- w_keyval: bfloat16 [2048, 2, 2048], P(None, None, 'tp'), may hold values from -30 to 30
- w_out: bfloat16 [2048, 2048], P('tp'), may hold values from -0.125 to 0.125
- w_gate_up: bfloat16 [2048, 2, 8192], P(None, None, 'tp'), may hold values from -0.125 to 0.125
- w_down: bfloat16 [8192, 2048], P('tp'), may hold values from -0.0625 to 0.0625
- root_cache: bfloat16 [8, 4096, 2, 2048], P(None, 'req', None, 'tp'), may hold values from -240 to 240
- mid_cache: bfloat16 [16, 2048, 2, 2048], P('req', None, None, 'tp'), may hold values from -240 to 240
- leaf_cache: bfloat16 [512, 128, 2, 2048], P('req', None, None, 'tp'), may hold values from -240 to 240
- held_hidden: bfloat16 [16, 256, 2048], P('req', None, 'tp'), may hold values from -6 to 6
- recompute_rows: int32 [16, 256], P('req'), may hold values from 0 to 2047, as said below
- root_len: int32 [8], replicated, may hold values from 1024 to 4096
- mid_len: int32 [16], replicated, may hold values from 256 to 2048
- leaf_len: int32 [512], P('req'), may hold values from 1 to 128
- mid_parent: int32 [16], replicated, may hold values from 0 to 7
- leaf_parent: int32 [512], replicated, may hold values from 0 to 15
Outputs:
- layer_out: bfloat16 [512, 2048], P('req', 'tp')
Inputs may be any that keep to these rules, and one draw needn't show every extreme that they name: `recompute_rows`: the 256 slots of one middle node are distinct.
All inputs are finite; a program needn't handle non-finite values.
Results may differ from a plain program's by a relative error of at most 0.02.
The roundings to bfloat16 on the way count: a program that leaves them out, or rounds other values in their place, can miss the bound.
Values may be sent and summed in bfloat16 or wider, within the bound.
A program may use at most 192 MiB of HBM per device.

v0:
```python
import math

import jax
import jax.numpy as jnp
from jax import lax
from jax.sharding import PartitionSpec as P

D = 2048
HEAD_DIM = 64


EPSILON = 1e-05
THETA_BASE = 130000.0
NEG_FILL = -1e30


def combined_all(value, axis, combine):
    everything = jax.tree.map(lambda part: lax.all_gather(part, axis), value)
    first = jax.tree.map(lambda part: part[0], everything)

    def lap(k, so_far):
        return combine(so_far, jax.tree.map(lambda part: part[k], everything))

    return lax.fori_loop(1, lax.axis_size(axis), lap, first)


def rms_scale(values, gain):
    return (
        values
        * lax.rsqrt(jnp.mean(values * values, axis=-1, keepdims=True) + EPSILON)
        * gain.astype(jnp.float32)
    )


def rotate(values, positions):
    half_dim = values.shape[-1] // 2
    inv_freq = jnp.exp(
        jnp.arange(half_dim, dtype=jnp.float32) * (-2.0 * math.log(THETA_BASE) / values.shape[-1])
    )
    angles = positions.astype(jnp.float32)[..., None, None] * inv_freq
    cosines = jnp.cos(angles)
    sines = jnp.sin(angles)
    leading = values[..., :half_dim]
    trailing = values[..., half_dim:]
    return jnp.concatenate(
        [leading * cosines - trailing * sines, trailing * cosines + leading * sines], axis=-1
    )


def lookup(table_values, indices):
    hits = indices[..., None] == jnp.arange(table_values.shape[0], dtype=jnp.int32)
    return jnp.sum(jnp.where(hits, table_values, 0), axis=-1)


def partial_softmax(queries, key_rows, live_mask, score_scale):
    count = key_rows.shape[0]
    heads = queries.shape[1]
    key_part = key_rows[:, 0].reshape(count, heads, HEAD_DIM)
    value_part = key_rows[:, 1].reshape(count, heads, HEAD_DIM)
    scores = (
        jnp.einsum("bhd,khd->hbk", queries, key_part, preferred_element_type=jnp.float32)
        * score_scale
    )
    live = live_mask[None]
    row_max = jnp.max(jnp.where(live, scores, NEG_FILL), axis=2)
    weights = jnp.where(live, jnp.exp(scores - row_max[..., None]), 0.0)
    row_sum = jnp.sum(weights, axis=2)
    weighted = jnp.einsum(
        "hbk,khd->bhd", weights.astype(jnp.bfloat16), value_part, preferred_element_type=jnp.float32
    )
    return (row_max.T, row_sum.T, weighted.reshape(queries.shape[0], heads * HEAD_DIM))


def join(earlier, latter):
    best = jnp.maximum(earlier[0], latter[0])
    factor_one = jnp.exp(earlier[0] - best)
    factor_two = jnp.exp(latter[0] - best)
    row_sum = earlier[1] * factor_one + latter[1] * factor_two
    weighted = earlier[2] * jnp.repeat(factor_one, HEAD_DIM, axis=1) + latter[2] * jnp.repeat(
        factor_two, HEAD_DIM, axis=1
    )
    return (best, row_sum, weighted)


def leaf_softmax(queries, leaf_cache, leaf_len, score_scale):
    own_rows, slots = leaf_cache.shape[:2]
    heads = queries.shape[1]
    key_part = leaf_cache[:, :, 0].reshape(own_rows, slots, heads, HEAD_DIM)
    value_part = leaf_cache[:, :, 1].reshape(own_rows, slots, heads, HEAD_DIM)
    scores = (
        jnp.einsum("rhd,rkhd->rhk", queries, key_part, preferred_element_type=jnp.float32)
        * score_scale
    )
    live = (jnp.arange(slots, dtype=jnp.int32)[None, :] < leaf_len[:, None])[:, None, :]
    row_max = jnp.max(jnp.where(live, scores, NEG_FILL), axis=2)
    weights = jnp.where(live, jnp.exp(scores - row_max[..., None]), 0.0)
    row_sum = jnp.sum(weights, axis=2)
    weighted = jnp.einsum(
        "rhk,rkhd->rhd",
        weights.astype(jnp.bfloat16),
        value_part,
        preferred_element_type=jnp.float32,
    )
    return (row_max, row_sum, weighted)


def on_device(
    stream,
    attn_gain,
    mlp_gain,
    w_query,
    w_keyval,
    w_out,
    w_gate_up,
    w_down,
    root_cache,
    mid_cache,
    leaf_cache,
    held_hidden,
    recompute_rows,
    root_len,
    mid_len,
    leaf_len,
    mid_parent,
    leaf_parent,
):
    req_rank = lax.axis_index("req")
    own_rows = stream.shape[0]
    query_width = w_query.shape[1]
    local_heads = query_width // HEAD_DIM
    score_scale = HEAD_DIM ** (-0.5)
    requests = leaf_parent.shape[0]
    all_roots = lookup(mid_parent, leaf_parent)
    own_mids = lax.dynamic_slice_in_dim(leaf_parent, req_rank * own_rows, own_rows)
    own_roots = lax.dynamic_slice_in_dim(all_roots, req_rank * own_rows, own_rows)
    positions = lookup(root_len, own_roots) + lookup(mid_len, own_mids) + leaf_len
    stream_float = stream.astype(jnp.float32)
    normed = rms_scale(stream_float, attn_gain).astype(jnp.bfloat16)
    keyval_flat = w_keyval.reshape(D, 2 * query_width)
    queries = rotate(
        jnp.dot(normed, w_query, preferred_element_type=jnp.float32).reshape(
            own_rows, local_heads, HEAD_DIM
        ),
        positions,
    ).astype(jnp.bfloat16)
    fresh = jnp.dot(normed, keyval_flat, preferred_element_type=jnp.float32).reshape(
        own_rows, 2, local_heads, HEAD_DIM
    )
    key_new = rotate(fresh[:, 0], positions).astype(jnp.bfloat16)
    value_new = fresh[:, 1].astype(jnp.bfloat16)
    node_count, slots = mid_cache.shape[:2]
    recomp_count = recompute_rows.shape[1]
    held = lax.all_gather(held_hidden, "tp", axis=2, tiled=True)
    held_normed = rms_scale(held.astype(jnp.float32), attn_gain).astype(jnp.bfloat16)
    rebuilt = jnp.dot(
        held_normed.reshape(node_count * recomp_count, D),
        keyval_flat,
        preferred_element_type=jnp.float32,
    ).reshape(node_count, recomp_count, 2, local_heads, HEAD_DIM)
    own_nodes = req_rank * node_count + jnp.arange(node_count, dtype=jnp.int32)
    own_lens = lax.dynamic_slice_in_dim(mid_len, req_rank * node_count, node_count)
    own_parents = lax.dynamic_slice_in_dim(mid_parent, req_rank * node_count, node_count)
    rebuilt_pos = lookup(root_len, own_parents)[:, None] + recompute_rows
    rebuilt = (
        jnp.stack([rotate(rebuilt[:, :, 0], rebuilt_pos), rebuilt[:, :, 1]], axis=2)
        .astype(jnp.bfloat16)
        .reshape(node_count * recomp_count, 2, query_width)
    )
    all_queries = lax.all_gather(
        queries.reshape(own_rows, query_width), "req", axis=0, tiled=True
    ).reshape(requests, local_heads, HEAD_DIM)
    root_count, slice_len = root_cache.shape[:2]
    token_ids = req_rank * slice_len + jnp.arange(slice_len, dtype=jnp.int32)
    root_valid = token_ids[None, :] < root_len[:, None]
    root_match = all_roots[:, None] == jnp.arange(root_count, dtype=jnp.int32)[None, :]
    root_mask = (root_match[:, :, None] & root_valid[None]).reshape(
        requests, root_count * slice_len
    )
    root_part = partial_softmax(
        all_queries,
        root_cache.reshape(root_count * slice_len, 2, query_width),
        root_mask,
        score_scale,
    )
    replaced = jnp.any(
        recompute_rows[:, :, None] == jnp.arange(slots, dtype=jnp.int32)[None, None, :], axis=1
    )
    slot_live = (jnp.arange(slots, dtype=jnp.int32)[None, :] < own_lens[:, None]) & jnp.logical_not(
        replaced
    )
    belongs = leaf_parent[:, None] == own_nodes[None, :]
    held_mask = (belongs[:, :, None] & slot_live[None]).reshape(requests, node_count * slots)
    fresh_mask = (belongs[:, :, None] & (recompute_rows < own_lens[:, None])[None]).reshape(
        requests, node_count * recomp_count
    )
    mid_keys = jnp.concatenate(
        [mid_cache.reshape(node_count * slots, 2, query_width), rebuilt], axis=0
    )
    mid_part = partial_softmax(
        all_queries, mid_keys, jnp.concatenate([held_mask, fresh_mask], axis=1), score_scale
    )
    part_max, part_sum, part_acc = join(root_part, mid_part)
    merged_max, merged_sum, merged_acc = combined_all((part_max, part_sum, part_acc), "req", join)
    remote_max = lax.dynamic_slice_in_dim(merged_max, req_rank * own_rows, own_rows, 0)[None]
    remote_sum = lax.dynamic_slice_in_dim(merged_sum, req_rank * own_rows, own_rows, 0)[None]
    remote_acc = lax.dynamic_slice_in_dim(merged_acc, req_rank * own_rows, own_rows, 0)[None]
    leaf_max, leaf_sum, leaf_acc = leaf_softmax(queries, leaf_cache, leaf_len, score_scale)
    self_score = (
        jnp.sum(queries.astype(jnp.float32) * key_new.astype(jnp.float32), axis=-1) * score_scale
    )
    best = jnp.maximum(jnp.maximum(jnp.max(remote_max, axis=0), leaf_max), self_score)
    remote_factor = jnp.exp(remote_max - best[None])
    leaf_factor = jnp.exp(leaf_max - best)
    self_factor = jnp.exp(self_score - best)
    row_sum = jnp.sum(remote_sum * remote_factor, axis=0) + leaf_sum * leaf_factor + self_factor
    sources = remote_acc.shape[0]
    weighted = jnp.sum(
        remote_acc.reshape(sources, own_rows, local_heads, HEAD_DIM) * remote_factor[..., None],
        axis=0,
    )
    weighted = (
        weighted
        + leaf_acc * leaf_factor[..., None]
        + value_new.astype(jnp.float32) * self_factor[..., None]
    )
    attended = (weighted / row_sum[..., None]).reshape(own_rows, query_width).astype(jnp.bfloat16)
    attn_part = jnp.dot(attended, w_out, preferred_element_type=jnp.float32)
    width_share = D // lax.axis_size("tp")
    tp_rank = lax.axis_index("tp")
    residual = stream_float + lax.psum(attn_part, "tp")
    mixed_in = rms_scale(residual, mlp_gain).astype(jnp.bfloat16)
    residual_share = lax.dynamic_slice_in_dim(residual, tp_rank * width_share, width_share, 1)
    hidden_width = w_gate_up.shape[2]
    projected = jnp.dot(
        mixed_in, w_gate_up.reshape(D, 2 * hidden_width), preferred_element_type=jnp.float32
    ).reshape(own_rows, 2, hidden_width)
    hidden = (jax.nn.silu(projected[:, 0]) * projected[:, 1]).astype(jnp.bfloat16)
    down_share = lax.psum_scatter(
        jnp.dot(hidden, w_down, preferred_element_type=jnp.float32),
        "tp",
        scatter_dimension=1,
        tiled=True,
    )
    return (residual_share + down_share).astype(jnp.bfloat16)


def solution(mesh):
    placed = (
        P("req", None),
        P(),
        P(),
        P(None, "tp"),
        P(None, None, "tp"),
        P("tp", None),
        P(None, None, "tp"),
        P("tp", None),
        P(None, "req", None, "tp"),
        P("req", None, None, "tp"),
        P("req", None, None, "tp"),
        P("req", None, "tp"),
        P("req", None),
        P(),
        P(),
        P("req"),
        P(),
        P(),
    )
    return jax.shard_map(
        on_device, mesh=mesh, in_specs=placed, out_specs=P("req", "tp"), check_vma=False
    )
```

profile of v0, /device:TPU:1, one launch (start us, length us, event | category | flops | bytes accessed | tf_op | source)
XLA Modules:
  0.0 367.4 jit_solution(2306715656610677094)
XLA Ops:
  18.7 2.5 copy.77
  21.2 2.9 fusion.44
  26.3 19.9 %all_gather.22 = bf16[512,256]{1,0:T(8,128)(2,1)S(1)} all-gather(bf16[32,256]{1,0:T(8,128)(2,1)S(1)} %convert_element_type.81), channel_id=1, replica_groups=mesh['req'=16,'tp'=8] {'req'}, dimensions={0}, use_global_device_ids=true | all-gather | bytes 278528 | tf_op jit(solution)/shard_map/all_gather | solution.py:169
  50.5 4.2 %fusion.81 = (bf16[2048,1,256]{2,1,0:T(2,128)(2,1)}, bf16[2048,1,256]{2,1,0:T(2,128)(2,1)}) fusion(bf16[2048,2,256]{2,1,0:T(2,128)(2,1)S(1)} %bitcast.183), kind=kLoop, calls=%fused_computation.143 | loop fusion | bytes 4194304 | tf_op jit(solution)/shard_map/slice | solution.py:59
  54.7 6.0 %copy.103 = bf16[2048,1,256]{0,2,1:T(8,128)(2,1)} copy(bf16[2048,1,256]{2,1,0:T(2,128)(2,1)} %get-tuple-element.234) | data formatting | bytes 2097152
  67.4 4.3 %copy.104 = bf16[2048,1,256]{0,2,1:T(8,128)(2,1)} copy(bf16[2048,1,256]{2,1,0:T(2,128)(2,1)S(1)} %copy-done.4) | data formatting | bytes 2097152
  73.8 2.5 pad_add_fusion
  76.2 4.5 %select_reduce_fusion.1 = (f32[4,512]{1,0:T(4,128)S(1)}, f32[4,512,2048]{2,1,0:T(8,128)S(1)}) fusion(pred[512,2048]{1,0:T(8,128)(4,1)S(1)} %broadcast_and_fusion.1, bf16[512,4,64]{0,2,1:T(8,128)(2,1)} %bitcast.189, bf16[2048,4,64]{0,2,1:T(8,128)(2,1)S(1)} %bitcast.188), kind=kOutput, calls=%fused_computation.13 | convolution fusion | flops 549451776 | bytes 19144704 | tf_op jit(solution)/shard_map/bhd,khd->hbk/dot_general | solution.py:61
  80.8 5.7 %copy-done.1 = f32[4,512,2048]{2,1,0:T(8,128)} copy-done((f32[4,512,2048]{2,1,0:T(8,128)}, f32[4,512,2048]{2,1,0:T(8,128)S(1)}, u32[]{:S(2)}) %copy-start.1) | copy-done | bytes 16777240
  86.4 5.2 %fusion.6 = f32[4,512]{1,0:T(4,128)} fusion(f32[4,512,2048]{2,1,0:T(8,128)S(1)} %get-tuple-element.253, f32[4,512]{1,0:T(4,128)S(1)} %get-tuple-element.252, pred[512,2048]{1,0:T(8,128)(4,1)S(1)} %broadcast_and_fusion.1), kind=kLoop, calls=%fused_computation.17 | loop fusion | flops 16775168 | bytes 17842176 | tf_op jit(solution)/shard_map/reduce_sum | solution.py:67
  93.2 2.8 convolution_bitcast_fusion
  96.4 13.3 %maximum_maximum_fusion = bf16[2304,2,256]{2,1,0:T(2,128)(2,1)S(1)} fusion(bf16[256,1,256]{2,1,0:T(2,128)(2,1)S(1)} %copy.79, bf16[256,1,256]{2,1,0:T(2,128)(2,1)S(1)} %copy.78, bf16[2048,2,256]{2,1,0:T(2,128)(2,1)} %bitcast.196), kind=kLoop, calls=%fused_computation.25 | loop fusion | flops 7077888 | bytes 4718592 | tf_op jit(solution)/shard_map/concatenate | solution.py:196
  109.7 4.8 %fusion.80 = (bf16[2304,1,256]{2,1,0:T(2,128)(2,1)}, bf16[2304,1,256]{2,1,0:T(2,128)(2,1)}) fusion(bf16[2304,2,256]{2,1,0:T(2,128)(2,1)S(1)} %maximum_maximum_fusion), kind=kLoop, calls=%fused_computation.142 | loop fusion | bytes 4718592 | tf_op jit(solution)/shard_map/slice | solution.py:59
  114.5 6.0 %copy.80 = bf16[2304,1,256]{0,2,1:T(8,128)(2,1)} copy(bf16[2304,1,256]{2,1,0:T(2,128)(2,1)} %get-tuple-element.232) | data formatting | bytes 2359296 | tf_op jit(solution)/shard_map/slice | solution.py:58
  120.6 6.0 %copy.82 = bf16[2304,1,256]{0,2,1:T(8,128)(2,1)} copy(bf16[2304,1,256]{2,1,0:T(2,128)(2,1)} %get-tuple-element.231) | data formatting | bytes 2359296 | tf_op jit(solution)/shard_map/slice | solution.py:59
  126.6 5.6 %select_reduce_fusion = (f32[4,512]{1,0:T(4,128)S(1)}, f32[4,512,2304]{2,1,0:T(8,128)S(1)}) fusion(pred[512,2304]{1,0:T(8,128)(4,1)} %pad_add_fusion, bf16[512,4,64]{0,2,1:T(8,128)(2,1)} %bitcast.190, bf16[2304,4,64]{0,2,1:T(8,128)(2,1)} %bitcast.187), kind=kOutput, calls=%fused_computation.11 | convolution fusion | flops 618133504 | bytes 21504000 | tf_op jit(solution)/shard_map/bhd,khd->hbk/dot_general | solution.py:61
  132.2 5.1 %fusion.4 = f32[4,512]{1,0:T(4,128)S(1)} fusion(f32[4,512,2304]{2,1,0:T(8,128)S(1)} %get-tuple-element.251, f32[4,512]{1,0:T(4,128)S(1)} %get-tuple-element.250, pred[512,2304]{1,0:T(8,128)(4,1)S(1)} %copy-done.2), kind=kLoop, calls=%fused_computation.15 | loop fusion | flops 18872320 | bytes 20070400 | tf_op jit(solution)/shard_map/reduce_sum | solution.py:67
  138.0 6.8 %fusion.29 = f32[512,4,64]{0,2,1:T(8,128)} fusion(bf16[2304,4,64]{0,2,1:T(8,128)(2,1)} %bitcast.197, f32[4,512,2304]{2,1,0:T(8,128)S(1)} %get-tuple-element.251, f32[4,512]{1,0:T(4,128)S(1)} %get-tuple-element.250, pred[512,2304]{1,0:T(8,128)(4,1)} %pad_add_fusion, f32[512,4]{0,1:T(4,128)} %get-tuple-element.228), kind=kOutput, calls=%fused_computation.38 | convolution fusion | flops 622985216 | bytes 21774336 | tf_op jit(solution)/shard_map/hbk,khd->bhd/dot_general | solution.py:68
  144.8 8.0 %fusion.26 = f32[512,4,64]{0,2,1:T(8,128)S(1)} fusion(f32[512,4,64]{0,2,1:T(8,128)} %fusion.29, bf16[2048,4,64]{0,2,1:T(8,128)(2,1)} %bitcast.198, f32[4,512,2048]{2,1,0:T(8,128)} %copy-done.1, f32[4,512]{1,0:T(4,128)S(1)} %copy-done.14, pred[512,2048]{1,0:T(8,128)(4,1)S(1)} %broadcast_and_fusion.1, f32[512,4]{0,1:T(4,128)S(1)} %get-tuple-element.227), kind=kOutput, calls=%fused_computation.37 | convolution fusion | flops 553910272 | bytes 19939328 | tf_op jit(solution)/shard_map/hbk,khd->bhd/dot_general | solution.py:68
  153.8 10.0 %fusion.79 = (bf16[32,128,1,256]{3,2,1,0:T(2,128)(2,1)}, bf16[32,128,1,256]{3,2,1,0:T(2,128)(2,1)}) fusion(bf16[32,128,2,256]{3,2,1,0:T(2,128)(2,1)} %param.30), kind=kLoop, calls=%fused_computation.141 | loop fusion | bytes 8388608 | tf_op jit(solution)/shard_map/slice | solution.py:88
  163.8 9.8 %copy.105 = bf16[32,128,1,256]{1,3,0,2:T(8,128)(2,1)} copy(bf16[32,128,1,256]{3,2,1,0:T(2,128)(2,1)} %get-tuple-element.229) | data formatting | bytes 4194304
  173.6 8.6 %copy.106 = bf16[32,128,1,256]{1,3,0,2:T(8,128)(2,1)S(1)} copy(bf16[32,128,1,256]{3,2,1,0:T(2,128)(2,1)} %get-tuple-element.230) | data formatting | bytes 4194304
  182.3 2.2 fusion.56
  186.0 18.8 %all-gather = f32[8192,4]{0,1:T(4,128)S(1)} all-gather(f32[512,4]{0,1:T(4,128)S(1)} %get-tuple-element.245), channel_id=2, replica_groups=mesh['req'=16,'tp'=8] {'req'}, dimensions={0}, use_global_device_ids=true | all-gather | bytes 139264 | tf_op jit(solution)/shard_map/all_gather | solution.py:18
  204.9 18.5 %all-gather.1 = f32[8192,4]{0,1:T(4,128)S(1)} all-gather(f32[512,4]{0,1:T(4,128)S(1)} %get-tuple-element.226), channel_id=3, replica_groups=mesh['req'=16,'tp'=8] {'req'}, dimensions={0}, use_global_device_ids=true | all-gather | bytes 139264 | tf_op jit(solution)/shard_map/all_gather | solution.py:18
  223.4 7.4 %all-gather.7.cloned.1.call-done = f32[16,512,256]{2,1,0:T(8,128)} async-done(((f32[1,512,256]{2,1,0:T(8,128)}), f32[16,512,256]{2,1,0:T(8,128)}) %all-gather.7.cloned.1.call-update) | async-done | bytes 8388624 | tf_op jit(solution)/shard_map/all_gather | solution.py:18
  232.1 23.7 %while.19 = (s32[]{:T(128)}, f32[512,4]{0,1:T(4,128)S(1)}, f32[512,4]{0,1:T(4,128)S(1)}, f32[512,256]{0,1:T(8,128)S(1)}, f32[16,512,4]{1,2,0:T(4,128)S(1)}, /*in...) while((s32[]{:T(128)}, f32[512,4]{0,1:T(4,128)S(1)}, ...), condition=%wide.region_12.13_spmd, body=%wide.region_11.12_spmd.sunk | while | flops 405509 | bytes 3752087 | solution.py:24
  258.3 10.1 %copy.110 = bf16[256,8,2,1024]{3,1,2,0:T(8,128)(2,1)} copy(bf16[256,8,2,1024]{3,2,1,0:T(2,128)(2,1)} %bitcast.182) | data formatting | bytes 16777216
  268.4 12.4 %copy.91 = bf16[2048,2048]{1,0:T(8,128)(2,1)} copy(bf16[2048,2048]{0,1:T(8,128)(2,1)} %bitcast.181) | data formatting | bytes 16777216 | tf_op jit(solution)/shard_map/dot_general | solution.py:234
  280.8 40.9 %all-reduce.2.cloned.1.call-done = f32[32,2048]{1,0:T(8,128)} async-done(((f32[32,2048]{1,0:T(8,128)}), f32[32,2048]{1,0:T(8,128)}) %all-reduce.2.cloned.1.call-update) | async-done | bytes 262160 | tf_op jit(solution)/shard_map/psum | solution.py:230
  322.8 6.1 %fusion.40 = f32[32,2,1024]{2,0,1:T(8,128)S(1)} fusion(bf16[2,1024,2048]{2,1,0:T(8,128)(2,1)} %bitcast.180, f32[32,2048]{1,0:T(8,128)S(1)} %get-tuple-element.219, f32[2048]{0:T(1024)S(1)} %convert_element_type.94, f32[32]{0:T(128)S(1)} %add_rsqrt_fusion.1), kind=kOutput, calls=%fused_computation.56 | convolution fusion | flops 268632064 | bytes 8921216 | tf_op jit(solution)/shard_map/dot_general | solution.py:234
  330.5 29.0 %reduce-scatter.2.cloned.1.call-done = f32[32,256]{1,0:T(8,128)} async-done(((f32[32,2048]{1,0:T(8,128)}), f32[32,256]{1,0:T(8,128)}) %reduce-scatter.2.cloned.1.call-update) | async-done | bytes 32784 | tf_op jit(solution)/shard_map/reduce_scatter | solution.py:238
  (184 shorter events, 63.4 us)
Async XLA Ops:
  6.5 250.7 %copy-start = (bf16[256,2048]{1,0:T(8,128)(2,1)S(1)}, bf16[256,2048]{1,0:T(8,128)(2,1)}, u32[]{:S(2)}) copy-start(bf16[256,2048]{1,0:T(8,128)(2,1)} %param.25) | copy-start | bytes 3145732
  6.5 85.1 %all-gather.5.cloned.1.call-start = ((), (), s32[]{:S(2)}) async-start(), calls=%async_computation.1 | async-start | bytes 1179648 | tf_op jit(solution)/shard_map/all_gather | solution.py:153
  7.3 223.6 %all-gather.7.cloned.1.call-start = ((), (), s32[]{:S(2)}) async-start(), calls=%async_computation.2 | async-start | bytes 8912896 | tf_op jit(solution)/shard_map/all_gather | solution.py:18
  16.6 4.6 %copy-start.7 = (bf16[32,2048]{1,0:T(8,128)(2,1)S(1)}, bf16[32,2048]{1,0:T(8,128)(2,1)}, u32[]{:S(2)}) copy-start(bf16[32,2048]{1,0:T(8,128)(2,1)} %param.20) | copy-start | bytes 393220
  18.7 5.4 %copy-start.21 = (s32[8]{0:T(128)S(1)}, s32[8]{0:T(128)}, u32[]{:S(2)}) copy-start(s32[8]{0:T(128)} %param.33) | copy-start | bytes 100
  18.7 5.5 %copy-start.19 = (s32[32]{0:T(128)S(1)}, s32[32]{0:T(128)}, u32[]{:S(2)}) copy-start(s32[32]{0:T(128)} %param.35) | copy-start | bytes 388
  21.2 29.3 %copy-start.3 = (bf16[8,256,2,256]{3,2,1,0:T(2,128)(2,1)S(1)}, bf16[8,256,2,256]{3,2,1,0:T(2,128)(2,1)}, u32[]{:S(2)}) copy-start(bf16[8,256,2,256]{3,2,1,0:T(2,128)(2,1)} %param.28) | copy-start | bytes 6291460
  24.1 0.7 copy-start.9
  25.6 0.6 copy-start.11
  50.5 11.5 %copy-start.18 = (s32[1,256]{1,0:T(1,128)S(1)}, s32[1,256]{1,0:T(1,128)}, u32[]{:S(2)}) copy-start(s32[1,256]{1,0:T(1,128)} %param.32) | copy-start | bytes 3076
  54.7 12.8 %copy-start.4 = (bf16[2048,1,256]{2,1,0:T(2,128)(2,1)S(1)}, bf16[2048,1,256]{2,1,0:T(2,128)(2,1)}, u32[]{:S(2)}) copy-start(bf16[2048,1,256]{2,1,0:T(2,128)(2,1)} %get-tuple-element.233) | copy-start | bytes 3145732
  71.7 4.5 %copy-start.5 = (bf16[2048,1,256]{0,2,1:T(8,128)(2,1)S(1)}, bf16[2048,1,256]{0,2,1:T(8,128)(2,1)}, u32[]{:S(2)}) copy-start(bf16[2048,1,256]{0,2,1:T(8,128)(2,1)} %copy.103) | copy-start | bytes 3145732
  80.7 5.7 %copy-start.1 = (f32[4,512,2048]{2,1,0:T(8,128)}, f32[4,512,2048]{2,1,0:T(8,128)S(1)}, u32[]{:S(2)}) copy-start(f32[4,512,2048]{2,1,0:T(8,128)S(1)} %get-tuple-element.253) | copy-start | bytes 50331652
  80.7 5.7 %copy-start.13 = (f32[4,512]{1,0:T(4,128)}, f32[4,512]{1,0:T(4,128)S(1)}, u32[]{:S(2)}) copy-start(f32[4,512]{1,0:T(4,128)S(1)} %get-tuple-element.252) | copy-start | bytes 24580
  91.6 4.3 %copy-start.10 = (f32[256,32]{0,1:T(8,128)S(1)}, f32[256,32]{0,1:T(8,128)}, u32[]{:S(2)}) copy-start(f32[256,32]{0,1:T(8,128)} %get-tuple-element.247) | copy-start | bytes 98308
  126.6 5.6 %copy-start.2 = (pred[512,2304]{1,0:T(8,128)(4,1)S(1)}, pred[512,2304]{1,0:T(8,128)(4,1)}, u32[]{:S(2)}) copy-start(pred[512,2304]{1,0:T(8,128)(4,1)} %pad_add_fusion) | copy-start | bytes 3538948
  132.2 5.1 %copy-start.14 = (f32[4,512]{1,0:T(4,128)S(1)}, f32[4,512]{1,0:T(4,128)}, u32[]{:S(2)}) copy-start(f32[4,512]{1,0:T(4,128)} %copy-done.13) | copy-start | bytes 24580
  132.2 5.1 %copy-start.15 = (f32[4,512]{1,0:T(4,128)S(1)}, f32[4,512]{1,0:T(4,128)}, u32[]{:S(2)}) copy-start(f32[4,512]{1,0:T(4,128)} %fusion.6) | copy-start | bytes 24580
  153.8 167.9 %all-reduce.2.cloned.1.call-start = ((), (), s32[]{:S(2)}) async-start(), calls=%async_computation.3 | async-start | bytes 524288 | tf_op jit(solution)/shard_map/psum | solution.py:230
  173.6 8.6 %copy-start.20 = (s32[32]{0:T(128)S(1)}, s32[32]{0:T(128)}, u32[]{:S(2)}) copy-start(s32[32]{0:T(128)} %param.35) | copy-start | bytes 388
  173.6 8.7 %copy-start.12 = (bf16[32,4,64]{2,0,1:T(8,128)(2,1)S(1)}, bf16[32,4,64]{2,0,1:T(8,128)(2,1)}, u32[]{:S(2)}) copy-start(bf16[32,4,64]{2,0,1:T(8,128)(2,1)} %copy-done.11) | copy-start | bytes 49156
  232.1 23.9 %copy-start.16 = (f32[32,4]{0,1:T(4,128)S(1)}, f32[32,4]{0,1:T(4,128)}, u32[]{:S(2)}) copy-start(f32[32,4]{0,1:T(4,128)} %get-tuple-element.224) | copy-start | bytes 1540
  258.2 101.3 %reduce-scatter.2.cloned.1.call-start = ((), (), s32[]{:S(2)}) async-start(), calls=%async_computation.4 | async-start | bytes 294912 | tf_op jit(solution)/shard_map/reduce_scatter | solution.py:238
  268.4 12.4 %copy-start.17 = (bf16[2048]{0:T(1024)(128)(2,1)S(1)}, bf16[2048]{0:T(1024)(128)(2,1)}, u32[]{:S(2)}) copy-start(bf16[2048]{0:T(1024)(128)(2,1)} %param.22) | copy-start | bytes 12292
  268.4 53.3 %copy-start.8 = (bf16[32,2048]{1,0:T(8,128)(2,1)S(1)}, bf16[32,2048]{1,0:T(8,128)(2,1)}, u32[]{:S(2)}) copy-start(bf16[32,2048]{1,0:T(8,128)(2,1)} %param.20) | copy-start | bytes 393220
  322.8 6.2 %copy-start.6 = (bf16[1024,2048]{1,0:T(8,128)(2,1)S(1)}, bf16[1024,2048]{1,0:T(8,128)(2,1)}, u32[]{:S(2)}) copy-start(bf16[1024,2048]{1,0:T(8,128)(2,1)} %param.27) | copy-start | bytes 12582916
Sparse Core Ops, SparseCore 0:
  9.0 27.1 all-gather.4
  153.9 76.8 all-gather.6
  258.3 63.2 all-reduce.1
  330.6 28.8 reduce-scatter.1
where the time goes:
time: 372 us; the launch traced here: 367 us
  local copies, waits for them, and re-layouts  124 us (33%)
  waiting for transfers between devices  78.1 us (21%)
  blocking collectives  57.3 us (15%)
  other arithmetic  50 us (13%)
  matrix products  44.2 us (12%)
  between operations  13.6 us (4%)
    unnamed x53, local copies, waits for them, and re-layouts  49.1 us
    psum x1, waiting for transfers between devices, on_device(): residual = stream_float + lax.psum(attn_part, 'tp')  40.9 us
    all_gather x2, blocking collectives, combined_all(): everything = jax.tree.map(lambda part: lax.all_gather(part, axis), value)  37.4 us
    reduce_scatter x1, waiting for transfers between devices, on_device(): lax.psum_scatter(jnp.dot(hidden, w_down, preferred_element_type=jnp.float...  29 us
    all_gather x1, blocking collectives, on_device(): lax.all_gather(queries.reshape(own_rows, query_width), 'req', axis=0, til...  19.9 us
    dynamic_slice x30, local copies, waits for them, and re-layouts, lap(): return combine(so_far, jax.tree.map(lambda part: part[k], everything))  19.2 us
    slice x3, local copies, waits for them, and re-layouts, partial_softmax(): value_part = key_rows[:, 1].reshape(count, heads, HEAD_DIM)  15 us
    dot_general x2, matrix products, partial_softmax(): jnp.einsum('hbk,khd->bhd', weights.astype(jnp.bfloat16), value_part, pref...  14.8 us
  transfers between devices with their start and end apart: 4, of which 3 were waited for; matrix products, arithmetic and copies ran while one was open for 31% of the time, Pallas kernels for 0%

commit v1 on v0

v1 whole, which is shorter than its diff:
```python
import math

import jax
import jax.numpy as jnp
import numpy as np
from jax import lax
from jax.experimental import pallas as pl
from jax.experimental.pallas import tpu as pltpu
from jax.sharding import PartitionSpec as P

F32 = jnp.float32
BF16 = jnp.bfloat16
I32 = jnp.int32
D = 2048
HEAD_DIM = 64
EPSILON = 1e-05
THETA_BASE = 130000.0
NEG_FILL = -1e30
NREQ = 16
NTP = 8
ROWS = 32
WIDTH = 256
HEADS = 4
BLOCK = 32
MAX_BLOCKS = 32
STATS = 128
MSG = WIDTH + STATS


def iota(shape, dim):
    return lax.broadcasted_iota(I32, shape, dim)


def dot(a, b):
    return jnp.dot(a, b, preferred_element_type=F32)


def dot_t(a, b):
    return lax.dot_general(a, b, (((1,), (1,)), ((), ())), preferred_element_type=F32)


def as_col(row):
    n = row.shape[1]
    eye = iota((n, n), 0) == iota((n, n), 1)
    return jnp.sum(jnp.where(eye, row, 0.0), axis=1, keepdims=True)


def as_row(col):
    n = col.shape[0]
    eye = iota((n, n), 0) == iota((n, n), 1)
    return jnp.sum(jnp.where(eye, col, 0.0), axis=0, keepdims=True)


def rope_tables(positions, inv_freq):
    angles = positions * inv_freq
    return jnp.cos(angles), jnp.sin(angles)


def rope(values, cosines, sines):
    n = values.shape[0]
    low = (iota((n, 128), 1) % 64) < 32
    parts = []
    for t in range(2):
        v = values[:, t * 128 : (t + 1) * 128]
        turned = jnp.where(low, -pltpu.roll(v, 96, 1), pltpu.roll(v, 32, 1))
        parts.append(v * cosines + turned * sines)
    return jnp.concatenate(parts, axis=1)


def shift_pairs(scores):
    width = scores.shape[1]
    return jnp.concatenate(
        [pltpu.roll(scores[:, i : i + 128], 1, 1) for i in range(0, width, 128)], axis=1
    )


def three_terms(values):
    first = values.astype(BF16)
    rest = values - first.astype(F32)
    second = rest.astype(BF16)
    third = (rest - second.astype(F32)).astype(BF16)
    return first, second, third


def project_kernel(
    stream_ref,
    gain_ref,
    wq_hbm,
    wkv_hbm,
    leaf_hbm,
    held_ref,
    lp_ref,
    mp_ref,
    rl_ref,
    ml_ref,
    ll_ref,
    rr_ref,
    freq_ref,
    qall_out,
    knew_out,
    vnew_out,
    oleaf_out,
    lleaf_out,
    wq_v,
    wkv_v,
    wk_v,
    wv_v,
    leaf_v,
    held_v,
    qall_v,
    qbd_v,
    score_v,
    acc_v,
    copy_sem,
    hsend,
    hrecv,
    qsend,
    qrecv,
):
    rank = lax.axis_index("req")
    tp = lax.axis_index("tp")
    barrier = pltpu.get_barrier_semaphore()
    for d in range(1, NREQ):
        pl.semaphore_signal(barrier, inc=1, device_id={"req": lax.rem(rank + d, NREQ)})
    for d in range(1, NTP):
        pl.semaphore_signal(barrier, inc=1, device_id={"tp": lax.rem(tp + d, NTP)})
    wq_copy = pltpu.make_async_copy(wq_hbm, wq_v, copy_sem.at[0])
    wkv_copy = pltpu.make_async_copy(wkv_hbm.reshape(2 * D, WIDTH), wkv_v, copy_sem.at[1])
    leaf_copy = pltpu.make_async_copy(leaf_hbm.reshape(8192, WIDTH), leaf_v, copy_sem.at[2])
    wq_copy.start()
    wkv_copy.start()
    leaf_copy.start()
    pl.semaphore_wait(barrier, NREQ + NTP - 2)
    held_copies = []
    for d in range(1, NTP):
        copy = pltpu.make_async_remote_copy(
            src_ref=held_ref,
            dst_ref=held_v.at[tp],
            send_sem=hsend.at[d],
            recv_sem=hrecv.at[d],
            device_id={"tp": lax.rem(tp + d, NTP)},
        )
        copy.start()
        held_copies.append(copy)
    held_v[tp] = held_ref[...]

    gain = gain_ref[...].astype(F32)
    x = stream_ref[...].astype(F32)
    normed = (
        x * lax.rsqrt(jnp.mean(x * x, axis=-1, keepdims=True) + EPSILON) * gain
    ).astype(BF16)

    lp_row = lp_ref[...]
    mp_col = as_col(mp_ref[...].astype(F32))
    ml_col = as_col(ml_ref[...].astype(F32))
    rl_row = rl_ref[...].astype(F32)
    parent_len = jnp.sum(
        jnp.where(iota((16, 8), 1).astype(F32) == mp_col, rl_row, 0.0), axis=1, keepdims=True
    )
    mid_base = parent_len + ml_col
    belongs = iota((16, 512), 0) == lp_row
    base_row = jnp.sum(jnp.where(belongs, mid_base, 0.0), axis=0, keepdims=True)
    own = iota((ROWS, 512), 1) == iota((ROWS, 512), 0) + rank * ROWS
    leaf_len_row = ll_ref[...].astype(F32)
    positions = jnp.sum(jnp.where(own, base_row, 0.0), axis=1, keepdims=True) + as_col(leaf_len_row)
    freq = freq_ref[...]
    cosines, sines = rope_tables(positions, freq)

    wq_copy.wait()
    queries = rope(dot(normed, wq_v[...]), cosines, sines).astype(BF16)
    queries = (queries.astype(F32) * (HEAD_DIM**-0.5)).astype(BF16)
    own_rows = pl.ds(pl.multiple_of(rank * ROWS, ROWS), ROWS)
    qall_v[own_rows, :] = queries
    q_copies = []
    for d in range(1, NREQ):
        copy = pltpu.make_async_remote_copy(
            src_ref=qall_v.at[own_rows],
            dst_ref=qall_v.at[own_rows],
            send_sem=qsend.at[d],
            recv_sem=qrecv.at[d],
            device_id={"req": lax.rem(rank + d, NREQ)},
        )
        copy.start()
        q_copies.append(copy)

    r2, c2 = iota((256, 256), 0), iota((256, 256), 1)
    split = (c2 == jnp.where(r2 < 128, 2 * r2, 2 * r2 - 255)).astype(BF16)
    wkv_copy.wait()
    for k in range(16):
        both = dot(split, wkv_v[k * 256 : (k + 1) * 256, :]).astype(BF16)
        wk_v[k * 128 : (k + 1) * 128, :] = both[:128]
        wv_v[k * 128 : (k + 1) * 128, :] = both[128:]
    key_new = rope(dot(normed, wk_v[...]), cosines, sines).astype(BF16)
    value_new = dot(normed, wv_v[...]).astype(BF16)

    repeat = (iota((256, ROWS), 0) // 8 == iota((256, ROWS), 1)).astype(BF16)
    head_mask = (r2 % 8) == (c2 // HEAD_DIM)
    qbd = jnp.where(head_mask, dot(repeat, queries), 0.0)
    qbd_v[...] = qbd.astype(BF16)
    self_score = jnp.sum(qbd * dot(repeat, key_new), axis=1, keepdims=True)
    live_len = jnp.sum(repeat.astype(F32) * leaf_len_row, axis=1, keepdims=True)
    leaf_copy.wait()
    for r in range(ROWS):
        score_v[r * 8 : (r + 1) * 8, :] = dot_t(
            qbd_v[r * 8 : (r + 1) * 8, :], leaf_v[r * 256 : (r + 1) * 256, :]
        )
    live = ((c2 % 2) == 1) & ((c2 // 2).astype(F32) < live_len)
    scores = jnp.where(live, shift_pairs(score_v[...]), NEG_FILL)
    best = jnp.maximum(jnp.max(scores, axis=1, keepdims=True), self_score)
    weights = jnp.exp(scores - best)
    self_weight = jnp.exp(self_score - best)
    row_sum = jnp.sum(weights, axis=1, keepdims=True) + self_weight
    qbd_v[...] = weights.astype(BF16)
    for r in range(ROWS):
        acc_v[r * 8 : (r + 1) * 8, :] = dot(
            qbd_v[r * 8 : (r + 1) * 8, :], leaf_v[r * 256 : (r + 1) * 256, :]
        )
    acc = acc_v[...] + self_weight.astype(BF16).astype(F32) * dot(repeat, value_new)
    acc = jnp.where(head_mask, acc / row_sum, 0.0)
    oleaf_out[...] = jnp.sum(acc.reshape(ROWS, 8, WIDTH), axis=1)
    lse = best + jnp.log(row_sum)
    spread = jnp.where((r2 % 8)[:, :STATS] == c2[:, :STATS], lse, 0.0)
    lleaf_out[...] = jnp.sum(spread.reshape(ROWS, 8, STATS), axis=1)

    held_pos = jnp.sum(
        jnp.where(iota((16, 1), 0) == rank, parent_len, 0.0), axis=0, keepdims=True
    ) + as_col(rr_ref[...].astype(F32))
    held_cos, held_sin = rope_tables(held_pos, freq)
    for copy in held_copies:
        copy.wait_recv()
    total = jnp.zeros((256, 1), F32)
    for c in range(NTP):
        part = held_v[c].astype(F32)
        total = total + jnp.sum(part * part, axis=1, keepdims=True)
    scale = lax.rsqrt(total * (1.0 / D) + EPSILON)
    keys = jnp.zeros((256, WIDTH), F32)
    values = jnp.zeros((256, WIDTH), F32)
    for c in range(NTP):
        part = (held_v[c].astype(F32) * scale * gain[:, c * 256 : (c + 1) * 256]).astype(BF16)
        keys = keys + dot(part, wk_v[c * 256 : (c + 1) * 256, :])
        values = values + dot(part, wv_v[c * 256 : (c + 1) * 256, :])
    knew_out[...] = rope(keys, held_cos, held_sin).astype(BF16)
    vnew_out[...] = values.astype(BF16)

    for copy in q_copies:
        copy.wait_recv()
    qall_out[...] = qall_v[...]
    for copy in held_copies:
        copy.wait_send()
    for copy in q_copies:
        copy.wait_send()


def attend_kernel(
    rl_s,
    ml_s,
    rank_s,
    qall_ref,
    root_hbm,
    mid_hbm,
    knew_ref,
    vnew_ref,
    lp_ref,
    mp_ref,
    rr_ref,
    out_ref,
    root_v,
    mid_v,
    qs_v,
    xs_v,
    bias_v,
    table_v,
    table_s,
    m_v,
    l_v,
    acc_v,
    copy_sem,
):
    rank = rank_s[0]
    root_copy = pltpu.make_async_copy(root_hbm.reshape(8, 512, WIDTH), root_v, copy_sem.at[0])
    mid_copy = pltpu.make_async_copy(mid_hbm.reshape(4096, WIDTH), mid_v, copy_sem.at[1])
    root_copy.start()
    mid_copy.start()
    belongs = iota((16, 512), 0) == lp_ref[...]
    belongs_f = belongs.astype(F32)
    before = (iota((512, 512), 0) < iota((512, 512), 1)).astype(BF16)
    order = dot(belongs_f.astype(BF16), before)
    counts = jnp.sum(belongs_f, axis=1, keepdims=True)
    blocks = jnp.floor((counts + (BLOCK - 1)) * (1.0 / BLOCK))
    start = jnp.sum(
        jnp.where(iota((16, 16), 1) < iota((16, 16), 0), as_row(blocks), 0.0), axis=1, keepdims=True
    )
    dest = jnp.sum(jnp.where(belongs, order + start * BLOCK, 0.0), axis=0, keepdims=True)
    lane = iota((16, 128), 1).astype(F32)
    node = jnp.sum((start + blocks <= lane).astype(F32), axis=0, keepdims=True)
    of_node = iota((16, 128), 0).astype(F32) == node
    mp_col = as_col(mp_ref[...].astype(F32))
    root = jnp.sum(jnp.where(of_node, mp_col, 0.0), axis=0, keepdims=True)
    used = jnp.sum(blocks, axis=0, keepdims=True)
    row8 = iota((8, 128), 0)
    table = jnp.where(row8 == 0, node, jnp.where(row8 == 1, root, used))
    table_v[...] = table.astype(I32)
    table_copy = pltpu.make_async_copy(table_v, table_s, copy_sem.at[2])
    table_copy.start()

    dest_i = dest.astype(I32)
    pick = (iota((MAX_BLOCKS * BLOCK, 512), 0) == dest_i).astype(BF16)
    qs_v[...] = dot(pick, qall_ref[...]).astype(BF16)
    xs_v[...] = jnp.zeros_like(xs_v)

    own_len = ml_s[rank]
    rr = rr_ref[...]
    slot_col = as_col(rr.astype(F32)).astype(I32)
    hit_hi = (iota((16, 256), 0) == rr // 128).astype(BF16)
    hit_lo = (iota((256, 256), 1) == 2 * (slot_col % 128) + 1).astype(BF16)
    replaced = dot(hit_hi, hit_lo)
    lane16 = iota((16, 256), 1)
    token = iota((16, 256), 0) * 128 + lane16 // 2
    alive = ((lane16 % 2) == 1) & (token < own_len) & (replaced < 0.5)
    bias_v[...] = jnp.where(alive, 0.0, NEG_FILL)
    new_bias = jnp.where(rr < own_len, 0.0, NEG_FILL)

    lane512 = iota((1, 512), 1)
    head_row = iota((128, WIDTH), 0) // BLOCK
    head_mask = (head_row == iota((128, WIDTH), 1) // HEAD_DIM).astype(BF16)
    lane_head = iota((BLOCK, WIDTH), 1) // HEAD_DIM
    lane128 = iota((BLOCK, STATS), 1)
    table_copy.wait()
    root_copy.wait()
    mid_copy.wait()
    n_blocks = table_s[2, 0]

    def update(scores, values):
        m_old = m_v[...]
        m_new = jnp.maximum(m_old, jnp.max(scores, axis=1, keepdims=True))
        fade = jnp.exp(m_old - m_new)
        weights = jnp.exp(scores - m_new)
        m_v[...] = m_new
        l_v[...] = l_v[...] * fade + jnp.sum(weights, axis=1, keepdims=True)
        acc_v[...] = acc_v[...] * fade + dot(weights.astype(BF16), values)

    def one_block(j, _):
        at = pl.ds(pl.multiple_of(j * BLOCK, BLOCK), BLOCK)
        q = qs_v[at, :]
        qbd = jnp.concatenate([q] * HEADS, axis=0) * head_mask
        node_j = table_s[0, j]
        root_j = table_s[1, j]
        pairs = root_v[root_j]
        live = ((lane512 % 2) == 1) & (rank * 256 + lane512 // 2 < rl_s[root_j])
        bias = jnp.where(live, 0.0, NEG_FILL)
        scores = shift_pairs(dot_t(qbd, pairs)) + bias
        m = jnp.max(scores, axis=1, keepdims=True)
        weights = jnp.exp(scores - m)
        m_v[...] = m
        l_v[...] = jnp.sum(weights, axis=1, keepdims=True)
        acc_v[...] = dot(weights.astype(BF16), pairs)

        @pl.when(node_j == rank)
        def _():
            for c in range(8):
                chunk = mid_v[c * 512 : (c + 1) * 512, :]
                bias_c = jnp.concatenate(
                    [bias_v[2 * c : 2 * c + 1, :], bias_v[2 * c + 1 : 2 * c + 2, :]], axis=1
                )
                update(shift_pairs(dot_t(qbd, chunk)) + bias_c, chunk)
            update(dot_t(qbd, knew_ref[...]) + new_bias, vnew_ref[...])

        l = l_v[...]
        out = acc_v[...] / l
        lse = m_v[...] + jnp.log(l)
        picked = jnp.zeros((BLOCK, WIDTH), F32)
        stats = jnp.zeros((BLOCK, STATS), F32)
        for h in range(HEADS):
            rows = slice(h * BLOCK, (h + 1) * BLOCK)
            picked = jnp.where(lane_head == h, out[rows], picked)
            stats = jnp.where((lane128 % 4) == h, lse[rows], stats)
        a, b, c = three_terms(stats)
        stats = jnp.where(
            lane128 < 4,
            a.astype(F32),
            jnp.where(lane128 < 8, b.astype(F32), jnp.where(lane128 < 12, c.astype(F32), 0.0)),
        )
        xs_v[at, :] = jnp.concatenate([picked, stats], axis=1).astype(BF16)
        return 0

    lax.fori_loop(0, n_blocks, one_block, 0)
    dest_col = as_col(dest).astype(I32)
    back = (iota((512, MAX_BLOCKS * BLOCK), 1) == dest_col).astype(BF16)
    out_ref[...] = dot(back, xs_v[...]).astype(BF16)


def finish_kernel(
    parts_ref,
    oleaf_ref,
    lleaf_ref,
    stream_ref,
    gain_ref,
    wout_hbm,
    wgu_hbm,
    wdn_hbm,
    out_ref,
    wout_v,
    wgu_v,
    wdn_v,
    in_v,
    rs_out,
    rs_in,
    ag_v,
    ds_out,
    ds_in,
    proj_v,
    copy_sem,
    asend,
    arecv,
    rsend,
    rrecv,
    gsend,
    grecv,
    dsend,
    drecv,
):
    rank = lax.axis_index("req")
    tp = lax.axis_index("tp")
    barrier = pltpu.get_barrier_semaphore()
    for d in range(1, NREQ):
        pl.semaphore_signal(barrier, inc=1, device_id={"req": lax.rem(rank + d, NREQ)})
    for d in range(1, NTP):
        pl.semaphore_signal(barrier, inc=1, device_id={"tp": lax.rem(tp + d, NTP)})
    wout_copy = pltpu.make_async_copy(wout_hbm, wout_v, copy_sem.at[0])
    wgu_copy = pltpu.make_async_copy(wgu_hbm.reshape(2 * D, 1024), wgu_v, copy_sem.at[1])
    wdn_copy = pltpu.make_async_copy(wdn_hbm, wdn_v, copy_sem.at[2])
    wout_copy.start()
    wgu_copy.start()
    wdn_copy.start()
    pl.semaphore_wait(barrier, NREQ + NTP - 2)
    copies = []
    for d in range(1, NREQ):
        peer = lax.rem(rank + d, NREQ)
        copy = pltpu.make_async_remote_copy(
            src_ref=parts_ref.at[pl.ds(pl.multiple_of(peer * ROWS, ROWS), ROWS)],
            dst_ref=in_v.at[d],
            send_sem=asend.at[d],
            recv_sem=arecv.at[d],
            device_id={"req": peer},
        )
        copy.start()
        copies.append(copy)
    in_v[0] = parts_ref[pl.ds(pl.multiple_of(rank * ROWS, ROWS), ROWS), :]
    i2, j2 = iota((256, 512), 0), iota((256, 512), 1)
    to_even = (j2 == 2 * i2).astype(BF16)
    to_odd = (j2 == 2 * i2 + 1).astype(BF16)
    e0, e1 = iota((STATS, WIDTH), 0), iota((STATS, WIDTH), 1)
    expand = ((e0 < 8) & ((e0 % 4) == e1 // HEAD_DIM)).astype(BF16)
    lane = iota((ROWS, STATS), 1)
    for copy in copies:
        copy.wait_recv()
    lses = []
    for s in range(NREQ):
        stats = in_v[s, :, WIDTH:].astype(F32)
        lses.append(stats + pltpu.roll(stats, 124, 1) + pltpu.roll(stats, 120, 1))
    lses.append(lleaf_ref[...])
    best = lses[0]
    for value in lses[1:]:
        best = jnp.maximum(best, value)
    shares = [jnp.exp(value - best) for value in lses]
    total = shares[0]
    for value in shares[1:]:
        total = total + value
    attended = jnp.zeros((ROWS, WIDTH), F32)
    for s in range(NREQ + 1):
        share = shares[s] / total
        first = share.astype(BF16)
        second = (share - first.astype(F32)).astype(BF16)
        both = jnp.where(
            lane < 4, first.astype(F32), jnp.where(lane < 8, pltpu.roll(second.astype(F32), 4, 1), 0.0)
        )
        factor = dot(both.astype(BF16), expand)
        source = in_v[s, :, :WIDTH].astype(F32) if s < NREQ else oleaf_ref[...]
        attended = attended + factor * source
    attended = attended.astype(BF16)

    wout_copy.wait()
    rs_copies = []
    for d in range(1, NTP):
        peer = lax.rem(tp + d, NTP)
        cols = pl.ds(pl.multiple_of(peer * WIDTH, WIDTH), WIDTH)
        rs_out[d] = dot(attended, wout_v[:, cols]).astype(BF16)
        copy = pltpu.make_async_remote_copy(
            src_ref=rs_out.at[d],
            dst_ref=rs_in.at[d],
            send_sem=rsend.at[d],
            recv_sem=rrecv.at[d],
            device_id={"tp": peer},
        )
        copy.start()
        rs_copies.append(copy)
    own_cols = pl.ds(pl.multiple_of(tp * WIDTH, WIDTH), WIDTH)
    residual = dot(attended, wout_v[:, own_cols]) + stream_ref[:, own_cols].astype(F32)
    for d in range(1, NTP):
        rs_copies[d - 1].wait_recv()
        residual = residual + rs_in[d].astype(F32)

    square = jnp.sum(residual * residual, axis=1, keepdims=True)
    a, b, c = three_terms(jnp.broadcast_to(square, (ROWS, STATS)))
    stats = jnp.where(
        lane == 0,
        a.astype(F32),
        jnp.where(lane == 1, b.astype(F32), jnp.where(lane == 2, c.astype(F32), 0.0)),
    )
    scaled = residual * gain_ref[:, own_cols].astype(F32)
    ag_v[0] = jnp.concatenate([scaled, stats], axis=1).astype(BF16)
    ag_copies = []
    for d in range(1, NTP):
        copy = pltpu.make_async_remote_copy(
            src_ref=ag_v.at[0],
            dst_ref=ag_v.at[d],
            send_sem=gsend.at[d],
            recv_sem=grecv.at[d],
            device_id={"tp": lax.rem(tp + d, NTP)},
        )
        copy.start()
        ag_copies.append(copy)
    wgu_copy.wait()
    squares = jnp.zeros((ROWS, STATS), F32)
    for d in range(NTP):
        if d > 0:
            ag_copies[d - 1].wait_recv()
        owner = lax.rem(tp + NTP - d, NTP)
        part = ag_v[d]
        squares = squares + part[:, WIDTH:].astype(F32)
        chunk = part[:, :WIDTH]
        mixed = jnp.concatenate([dot(chunk, to_even), dot(chunk, to_odd)], axis=0).astype(BF16)
        rows = pl.ds(pl.multiple_of(owner * 512, 512), 512)
        for n in range(4):
            cols = slice(n * 256, (n + 1) * 256)
            product = dot(mixed, wgu_v[rows, cols])
            if d == 0:
                proj_v[:, cols] = product
            else:
                proj_v[:, cols] += product
    mean = jnp.sum(squares, axis=1, keepdims=True) * (1.0 / D)
    scale = lax.rsqrt(mean + EPSILON)
    gate = proj_v[:ROWS, :] * scale
    up = proj_v[ROWS:, :] * scale
    hidden = (gate / (1.0 + jnp.exp(-gate)) * up).astype(BF16)

    wdn_copy.wait()
    ds_copies = []
    for d in range(1, NTP):
        peer = lax.rem(tp + d, NTP)
        cols = pl.ds(pl.multiple_of(peer * WIDTH, WIDTH), WIDTH)
        ds_out[d] = dot(hidden, wdn_v[:, cols]).astype(BF16)
        copy = pltpu.make_async_remote_copy(
            src_ref=ds_out.at[d],
            dst_ref=ds_in.at[d],
            send_sem=dsend.at[d],
            recv_sem=drecv.at[d],
            device_id={"tp": peer},
        )
        copy.start()
        ds_copies.append(copy)
    result = residual + dot(hidden, wdn_v[:, own_cols])
    for d in range(1, NTP):
        ds_copies[d - 1].wait_recv()
        result = result + ds_in[d].astype(F32)
    out_ref[...] = result.astype(BF16)
    for copy in copies + rs_copies + ag_copies + ds_copies:
        copy.wait_send()


VMEM = pl.BlockSpec(memory_space=pltpu.VMEM)
SMEM = pl.BlockSpec(memory_space=pltpu.SMEM)
ANY = pl.BlockSpec(memory_space=pl.ANY)
DMA = pltpu.SemaphoreType.DMA
LIMIT = 48 * 1024 * 1024


def on_device(
    stream,
    attn_gain,
    mlp_gain,
    w_query,
    w_keyval,
    w_out,
    w_gate_up,
    w_down,
    root_cache,
    mid_cache,
    leaf_cache,
    held_hidden,
    recompute_rows,
    root_len,
    mid_len,
    leaf_len,
    mid_parent,
    leaf_parent,
):
    freq = np.exp(np.arange(32, dtype=np.float32) * np.float32(-2.0 * math.log(THETA_BASE) / HEAD_DIM))
    freq = jnp.asarray(np.tile(freq.astype(np.float32), 4)[None, :])
    lp = leaf_parent.reshape(1, 512)
    mp = mid_parent.reshape(1, 16)
    qall, knew, vnew, oleaf, lleaf = pl.pallas_call(
        project_kernel,
        name="project",
        out_shape=(
            jax.ShapeDtypeStruct((512, WIDTH), BF16),
            jax.ShapeDtypeStruct((256, WIDTH), BF16),
            jax.ShapeDtypeStruct((256, WIDTH), BF16),
            jax.ShapeDtypeStruct((ROWS, WIDTH), F32),
            jax.ShapeDtypeStruct((ROWS, STATS), F32),
        ),
        in_specs=[VMEM, VMEM, ANY, ANY, ANY] + [VMEM] * 8,
        out_specs=(VMEM,) * 5,
        scratch_shapes=[
            pltpu.VMEM((D, WIDTH), BF16),
            pltpu.VMEM((2 * D, WIDTH), BF16),
            pltpu.VMEM((D, WIDTH), BF16),
            pltpu.VMEM((D, WIDTH), BF16),
            pltpu.VMEM((8192, WIDTH), BF16),
            pltpu.VMEM((NTP, 256, 256), BF16),
            pltpu.VMEM((512, WIDTH), BF16),
            pltpu.VMEM((256, WIDTH), BF16),
            pltpu.VMEM((256, WIDTH), F32),
            pltpu.VMEM((256, WIDTH), F32),
            DMA((3,)),
            DMA((NTP,)),
            DMA((NTP,)),
            DMA((NREQ,)),
            DMA((NREQ,)),
        ],
        compiler_params=pltpu.CompilerParams(
            collective_id=0, has_side_effects=True, vmem_limit_bytes=LIMIT
        ),
    )(
        stream,
        attn_gain.reshape(1, D),
        w_query,
        w_keyval,
        leaf_cache,
        held_hidden.reshape(256, 256),
        lp,
        mp,
        root_len.reshape(1, 8),
        mid_len.reshape(1, 16),
        leaf_len.reshape(1, ROWS),
        recompute_rows,
        freq,
    )
    rank = lax.axis_index("req").reshape(1).astype(I32)
    parts = pl.pallas_call(
        attend_kernel,
        name="attend",
        out_shape=jax.ShapeDtypeStruct((512, MSG), BF16),
        in_specs=[SMEM, SMEM, SMEM, VMEM, ANY, ANY] + [VMEM] * 5,
        out_specs=VMEM,
        scratch_shapes=[
            pltpu.VMEM((8, 512, WIDTH), BF16),
            pltpu.VMEM((4096, WIDTH), BF16),
            pltpu.VMEM((MAX_BLOCKS * BLOCK, WIDTH), BF16),
            pltpu.VMEM((MAX_BLOCKS * BLOCK, MSG), BF16),
            pltpu.VMEM((16, 256), F32),
            pltpu.VMEM((8, 128), I32),
            pltpu.SMEM((8, 128), I32),
            pltpu.VMEM((128, 1), F32),
            pltpu.VMEM((128, 1), F32),
            pltpu.VMEM((128, WIDTH), F32),
            DMA((3,)),
        ],
        compiler_params=pltpu.CompilerParams(vmem_limit_bytes=LIMIT),
    )(
        root_len,
        mid_len,
        rank,
        qall,
        root_cache,
        mid_cache,
        knew,
        vnew,
        lp,
        mp,
        recompute_rows,
    )
    return pl.pallas_call(
        finish_kernel,
        name="finish",
        out_shape=jax.ShapeDtypeStruct((ROWS, WIDTH), BF16),
        in_specs=[VMEM] * 5 + [ANY] * 3,
        out_specs=VMEM,
        scratch_shapes=[
            pltpu.VMEM((WIDTH, D), BF16),
            pltpu.VMEM((2 * D, 1024), BF16),
            pltpu.VMEM((1024, D), BF16),
            pltpu.VMEM((NREQ, ROWS, MSG), BF16),
            pltpu.VMEM((NTP, ROWS, WIDTH), BF16),
            pltpu.VMEM((NTP, ROWS, WIDTH), BF16),
            pltpu.VMEM((NTP, ROWS, MSG), BF16),
            pltpu.VMEM((NTP, ROWS, WIDTH), BF16),
            pltpu.VMEM((NTP, ROWS, WIDTH), BF16),
            pltpu.VMEM((2 * ROWS, 1024), F32),
            DMA((3,)),
            DMA((NREQ,)),
            DMA((NREQ,)),
            DMA((NTP,)),
            DMA((NTP,)),
            DMA((NTP,)),
            DMA((NTP,)),
            DMA((NTP,)),
            DMA((NTP,)),
        ],
        compiler_params=pltpu.CompilerParams(
            collective_id=1, has_side_effects=True, vmem_limit_bytes=LIMIT
        ),
    )(
        parts,
        oleaf,
        lleaf,
        stream,
        mlp_gain.reshape(1, D),
        w_out,
        w_gate_up,
        w_down,
    )


def solution(mesh):
    placed = (
        P("req", None),
        P(),
        P(),
        P(None, "tp"),
        P(None, None, "tp"),
        P("tp", None),
        P(None, None, "tp"),
        P("tp", None),
        P(None, "req", None, "tp"),
        P("req", None, None, "tp"),
        P("req", None, None, "tp"),
        P("req", None, "tp"),
        P("req", None),
        P(),
        P(),
        P("req"),
        P(),
        P(),
    )
    return jax.shard_map(
        on_device, mesh=mesh, in_specs=placed, out_specs=P("req", "tp"), check_vma=False
    )
```

time: 372 us -> 97.8 us (0.26); the launches traced: 367 us -> 97.4 us
  local copies, waits for them, and re-layouts: 124 us -> 19.5 us
  waiting for transfers between devices: 78.1 us -> 0 us
  Pallas kernels: 0 us -> 77.7 us
  blocking collectives: 57.3 us -> 0 us
  other arithmetic: 50 us -> 0 us
  matrix products: 44.2 us -> 0 us
  between operations: 13.6 us -> 0.11 us
    pallas_call x0 -> x3, Pallas kernels: none -> 77.7 us  [the longest x1 28.3 us: on_device(): pl.pallas_call(finish_kernel, name='finish', out_shape=jax.ShapeDtypeStru...]
    all_gather x3 -> x0, blocking collectives: 57.3 us -> none  [the longest x2 37.4 us: combined_all(): everything = jax.tree.map(lambda part: lax.all_gather(part, axis), value)]
    dot_general x12 -> x0, matrix products: 44.2 us -> none  [the longest x2 14.8 us: partial_softmax(): jnp.einsum('hbk,khd->bhd', weights.astype(jnp.bfloat16), value_part, pref...]
    psum x1 -> x0, waiting for transfers between devices: 40.9 us -> none  [on_device(): residual = stream_float + lax.psum(attn_part, 'tp')]
    slice x9 -> x0, local copies, waits for them, and re-layouts: 31.2 us -> none  [the longest x3 15 us: partial_softmax(): value_part = key_rows[:, 1].reshape(count, heads, HEAD_DIM)]
    unnamed x53 -> x57, local copies, waits for them, and re-layouts: 49.1 us -> 18.8 us
    reduce_scatter x1 -> x0, waiting for transfers between devices: 29 us -> none  [on_device(): lax.psum_scatter(jnp.dot(hidden, w_down, preferred_element_type=jnp.float...]
    dynamic_slice x35 -> x0, local copies, waits for them, and re-layouts: 22.6 us -> none  [the longest x30 19.2 us: lap(): return combine(so_far, jax.tree.map(lambda part: part[k], everything))]
  transfers between devices with their start and end apart: 4 -> 0, of which waited for: 3 -> 0; matrix products, arithmetic and copies ran while one was open for 31% -> 0% of each run, Pallas kernels for 0% -> 0%
where the time goes in v1:
time: 97.8 us; the launch traced here: 97.4 us
  Pallas kernels  77.7 us (79%)
  local copies, waits for them, and re-layouts  19.5 us (20%)
    pallas_call x1, Pallas kernels, on_device(): pl.pallas_call(finish_kernel, name='finish', out_shape=jax.ShapeDtypeStru...  28.3 us
    pallas_call x1, Pallas kernels, on_device(): pl.pallas_call(attend_kernel, name='attend', out_shape=jax.ShapeDtypeStru...  25.6 us
    pallas_call x1, Pallas kernels, on_device(): pl.pallas_call(project_kernel, name='project', out_shape=(jax.ShapeDtypeS...  23.8 us
    unnamed x57, local copies, waits for them, and re-layouts  18.8 us

profile of v1, /device:TPU:1, one launch (start us, length us, event | category | flops | bytes accessed | tf_op | source)
XLA Modules:
  0.0 97.4 jit_solution(585368783582633962)
XLA Ops:
  0.0 0.7 reshape.28.gain_ref
  0.7 1.6 %copy-done.1 = bf16[2048,2,256]{2,1,0:T(2,128)(2,1)S(1)} copy-done((bf16[2048,2,256]{2,1,0:T(2,128)(2,1)S(1)}, bf16[2048,2,256]{2,1,0:T(2,128)(2,1)}, u32[]{:S(2)}) %copy-start.1) | copy-done | bytes 2097176
  2.3 1.2 %copy-done.5 = bf16[2048,256]{1,0:T(8,128)(2,1)S(1)} copy-done((bf16[2048,256]{1,0:T(8,128)(2,1)S(1)}, bf16[2048,256]{1,0:T(8,128)(2,1)}, u32[]{:S(2)}) %copy-start.5) | copy-done | bytes 1048600
  3.5 0.9 copy-done.6
  4.4 0.9 copy-done.8
  5.3 0.7 copy-done.15
  6.0 0.7 copy-done.17
  6.7 0.7 copy-done.19
  7.3 0.7 copy-done.21
  8.0 0.7 copy-done.23
  8.7 0.7 copy-done.25
  9.3 0.7 copy-done.26
  10.0 23.8 %project.1 = (bf16[512,256]{1,0:T(8,128)(2,1)S(1)}, bf16[256,256]{1,0:T(8,128)(2,1)S(1)}, bf16[256,256]{1,0:T(8,128)(2,1)S(1)}, f32[32,256]{1,0:T(8,128)S(1)}, f32[32,128]{1,0:T(8,128)S(1)}) custom-call(bf16[32,2048]{1,0:T(8,128)(2,1)S(1)} %copy-done.6, bf16[1,2048]{1,0:T(2,128)(2,1)S(1)} %reshape.28.gain_ref, bf16[2048,256]{1,0:T(8,128)(2,1)S(1)} %copy-done.5, ...), custom_call_target="tpu_custom_call" | custom-call | tf_op jit(solution)/shard_map/project/pallas_call | solution.py:602
  33.8 0.0 copy-start.9
  33.8 0.7 copy-done.9
  34.5 0.6 copy-done.11
  35.1 0.6 copy-done.13
  35.8 0.0 copy-done.2
  35.8 1.7 %copy-done.3 = bf16[1,2048,2,256]{3,2,1,0:T(2,128)(2,1)S(1)} copy-done((bf16[1,2048,2,256]{3,2,1,0:T(2,128)(2,1)S(1)}, bf16[1,2048,2,256]{3,2,1,0:T(2,128)(2,1)}, u32[]{:S(2)}) %copy-start.3) | copy-done | bytes 2097176
  37.5 1.0 %copy-done.10 = bf16[256,256]{1,0:T(8,128)(2,1)S(1)} copy-done((bf16[256,256]{1,0:T(8,128)(2,1)S(1)}, bf16[256,256]{1,0:T(8,128)(2,1)}, u32[]{:S(2)}) %copy-start.10) | copy-done | bytes 131096
  38.5 0.9 copy-done.12
  39.5 0.7 copy-done.16
  40.1 0.7 copy-done.18
  40.8 0.7 copy-done.20
  41.5 0.7 copy-done.22
  42.1 0.7 copy-done.24
  42.8 25.6 %attend.1.parts_ref = bf16[512,384]{1,0:T(8,128)(2,1)S(1)} custom-call(s32[8]{0:T(128)S(1)} %copy-done.20, s32[16]{0:T(128)S(1)} %copy-done.22, s32[1]{0:T(128)} %bitcast.rank_s, bf16[512,256]{1,0:T(8,128)(2,1)S(1)} %get-tuple-element.10.qall_ref, bf16[8,256,2,256]{3,2,1,0:T(2,128)(2,1)S(1)} %copy-done.2, bf16[1,2048,2,256]{3,2,1,0:T(2,128)(2,1)S(1)} %copy-done.3, ...), custom_call_target="tpu_custom_call" | custom-call | tf_op jit(solution)/shard_map/attend/pallas_call | solution.py:650
  68.4 0.0 copy-done.27
  68.4 0.0 copy-done.4
  68.4 0.0 copy-done.7
  68.4 28.3 %finish.1 = bf16[32,256]{1,0:T(8,128)(2,1)S(1)} custom-call(bf16[512,384]{1,0:T(8,128)(2,1)S(1)} %attend.1.parts_ref, f32[32,256]{1,0:T(8,128)S(1)} %copy-done.14, f32[32,128]{1,0:T(8,128)S(1)} %get-tuple-element.14.lleaf_ref, bf16[32,2048]{1,0:T(8,128)(2,1)S(1)} %copy-done.7, bf16[1,2048]{1,0:T(2,128)(2,1)S(1)} %reshape.35.gain_ref, ...), custom_call_target="tpu_custom_call" | custom-call | tf_op jit(solution)/shard_map/finish/pallas_call | solution.py:683
  96.7 0.6 copy.21
  (30 shorter events, 0.1 us)
Async XLA Ops:
  0.7 1.6 %copy-start.1 = (bf16[2048,2,256]{2,1,0:T(2,128)(2,1)S(1)}, bf16[2048,2,256]{2,1,0:T(2,128)(2,1)}, u32[]{:S(2)}) copy-start(bf16[2048,2,256]{2,1,0:T(2,128)(2,1)} %wkv_hbm.1) | copy-start | bytes 6291460
  2.3 1.2 %copy-start.5 = (bf16[2048,256]{1,0:T(8,128)(2,1)S(1)}, bf16[2048,256]{1,0:T(8,128)(2,1)}, u32[]{:S(2)}) copy-start(bf16[2048,256]{1,0:T(8,128)(2,1)} %wq_hbm.1) | copy-start | bytes 3145732
  3.5 0.9 copy-start.6
  4.4 0.9 copy-start.8
  5.3 0.7 copy-start.15
  6.0 0.7 copy-start.17
  6.7 0.7 copy-start.19
  7.3 0.7 copy-start.21
  8.0 0.7 copy-start.23
  8.6 0.7 copy-start.25
  9.3 0.7 copy-start.26
  10.0 25.8 %copy-start.2 = (bf16[8,256,2,256]{3,2,1,0:T(2,128)(2,1)S(1)}, bf16[8,256,2,256]{3,2,1,0:T(2,128)(2,1)}, u32[]{:S(2)}) copy-start(bf16[8,256,2,256]{3,2,1,0:T(2,128)(2,1)} %root_hbm.1) | copy-start | bytes 6291460
  10.0 58.4 %copy-start.4 = (bf16[256,2048]{1,0:T(8,128)(2,1)S(1)}, bf16[256,2048]{1,0:T(8,128)(2,1)}, u32[]{:S(2)}) copy-start(bf16[256,2048]{1,0:T(8,128)(2,1)} %wout_hbm.1) | copy-start | bytes 3145732
  10.0 58.4 %copy-start.7 = (bf16[32,2048]{1,0:T(8,128)(2,1)S(1)}, bf16[32,2048]{1,0:T(8,128)(2,1)}, u32[]{:S(2)}) copy-start(bf16[32,2048]{1,0:T(8,128)(2,1)} %stream_ref.3) | copy-start | bytes 393220
  33.8 0.7 copy-start.9
  34.5 0.6 copy-start.11
  35.1 0.6 copy-start.13
  35.7 32.7 %copy-start = (bf16[1024,2048]{1,0:T(8,128)(2,1)S(1)}, bf16[1024,2048]{1,0:T(8,128)(2,1)}, u32[]{:S(2)}) copy-start(bf16[1024,2048]{1,0:T(8,128)(2,1)} %wdn_hbm.1) | copy-start | bytes 12582916
  35.8 1.7 %copy-start.3 = (bf16[1,2048,2,256]{3,2,1,0:T(2,128)(2,1)S(1)}, bf16[1,2048,2,256]{3,2,1,0:T(2,128)(2,1)}, u32[]{:S(2)}) copy-start(bf16[1,2048,2,256]{3,2,1,0:T(2,128)(2,1)} %mid_hbm.1) | copy-start | bytes 6291460
  37.5 1.0 %copy-start.10 = (bf16[256,256]{1,0:T(8,128)(2,1)S(1)}, bf16[256,256]{1,0:T(8,128)(2,1)}, u32[]{:S(2)}) copy-start(bf16[256,256]{1,0:T(8,128)(2,1)} %copy-done.9) | copy-start | bytes 393220
  38.5 0.9 copy-start.12
  39.5 0.7 copy-start.16
  40.1 0.7 copy-start.18
  40.8 0.7 copy-start.20
  41.5 0.7 copy-start.22
  42.1 0.7 copy-start.24
  42.8 25.6 %copy-start.27 = (bf16[2048]{0:T(1024)(128)(2,1)S(1)}, bf16[2048]{0:T(1024)(128)(2,1)}, u32[]{:S(2)}) copy-start(bf16[2048]{0:T(1024)(128)(2,1)} %param.21) | copy-start | bytes 12292
  42.8 25.6 %copy-start.14 = (f32[32,256]{1,0:T(8,128)S(1)}, f32[32,256]{1,0:T(8,128)}, u32[]{:S(2)}) copy-start(f32[32,256]{1,0:T(8,128)} %copy-done.13) | copy-start | bytes 98308

commit v2 on v0

v2 whole, which is shorter than its diff:
```python
import functools
import math

import jax
import jax.numpy as jnp
import numpy as np
from jax import lax
from jax.experimental import pallas as pl
from jax.experimental.pallas import tpu as pltpu
from jax.sharding import PartitionSpec as P

F32 = jnp.float32
BF16 = jnp.bfloat16
I32 = jnp.int32
D = 2048
HEAD_DIM = 64
EPSILON = 1e-05
THETA_BASE = 130000.0
NEG_FILL = -1e30
NREQ = 16
NTP = 8
ROWS = 32
WIDTH = 256
HEADS = 4
BLOCK = 32
BLOCKS = 24
SORTED = BLOCKS * BLOCK
MID_ROWS = 64
STATS = 128
MSG = WIDTH + STATS


def iota(shape, dim):
    return lax.broadcasted_iota(I32, shape, dim)


def dot(a, b):
    return jnp.dot(a, b, preferred_element_type=F32)


def dot_t(a, b):
    return lax.dot_general(a, b, (((1,), (1,)), ((), ())), preferred_element_type=F32)


def as_col(row):
    n = row.shape[1]
    eye = iota((n, n), 0) == iota((n, n), 1)
    return jnp.sum(jnp.where(eye, row, 0.0), axis=1, keepdims=True)


def as_row(col):
    n = col.shape[0]
    eye = iota((n, n), 0) == iota((n, n), 1)
    return jnp.sum(jnp.where(eye, col, 0.0), axis=0, keepdims=True)


def rope_tables(positions, inv_freq):
    angles = positions * inv_freq
    return jnp.cos(angles), jnp.sin(angles)


def rope(values, cosines, sines):
    n = values.shape[0]
    low = (iota((n, 128), 1) % 64) < 32
    parts = []
    for t in range(2):
        v = values[:, t * 128 : (t + 1) * 128]
        turned = jnp.where(low, -pltpu.roll(v, 96, 1), pltpu.roll(v, 32, 1))
        parts.append(v * cosines + turned * sines)
    return jnp.concatenate(parts, axis=1)


def shift_pairs(scores):
    width = scores.shape[1]
    return jnp.concatenate(
        [pltpu.roll(scores[:, i : i + 128], 1, 1) for i in range(0, width, 128)], axis=1
    )


def three_terms(values):
    first = values.astype(BF16)
    rest = values - first.astype(F32)
    second = rest.astype(BF16)
    third = (rest - second.astype(F32)).astype(BF16)
    return first, second, third


def total(values, axis):
    return jnp.sum(values, axis=axis, keepdims=True)


def head_columns(stacked, rows, width):
    lanes = iota((rows, width), 1)
    group = lanes // HEAD_DIM if width == WIDTH else lanes % HEADS
    picked = jnp.broadcast_to(stacked[:rows], (rows, width))
    for h in range(1, HEADS):
        picked = jnp.where(group == h, stacked[h * rows : (h + 1) * rows], picked)
    return picked


def packed(out, lse):
    lanes = iota(lse.shape, 1)
    a, b, c = three_terms(lse)
    stats = jnp.where(
        lanes < 4,
        a.astype(F32),
        jnp.where(lanes < 8, b.astype(F32), jnp.where(lanes < 12, c.astype(F32), 0.0)),
    )
    return jnp.concatenate([out, stats], axis=1).astype(BF16)


def unpacked_lse(stats):
    return stats + pltpu.roll(stats, 124, 1) + pltpu.roll(stats, 120, 1)


def split_pairs(split, pairs_v, first_v, second_v, tiles):
    for k in range(tiles):
        both = dot(split, pairs_v[k * 256 : (k + 1) * 256, :]).astype(BF16)
        first_v[k * 128 : (k + 1) * 128, :] = both[:128]
        second_v[k * 128 : (k + 1) * 128, :] = both[128:]


SMALL = (
    ((ROWS, D), BF16),
    ((D,), BF16),
    ((D,), BF16),
    ((512,), I32),
    ((16,), I32),
    ((8,), I32),
    ((16,), I32),
    ((ROWS,), I32),
    ((1, 256), I32),
    ((1, 128), F32),
)
WORK = dict(
    wq=((D, WIDTH), BF16),
    wkv=((2 * D, WIDTH), BF16),
    wk=((D, WIDTH), BF16),
    wv=((D, WIDTH), BF16),
    wout=((WIDTH, D), BF16),
    wgu=((2 * D, 1024), BF16),
    wdn=((1024, D), BF16),
    root=((4096, WIDTH), BF16),
    root_k=((8, 256, WIDTH), BF16),
    root_v=((8, 256, WIDTH), BF16),
    root_bias=((8, 1, 256), F32),
    mid=((4096, WIDTH), BF16),
    mid_k=((2048, WIDTH), BF16),
    mid_v=((2048, WIDTH), BF16),
    mid_bias=((16, 128), F32),
    leaf=((8192, WIDTH), BF16),
    held=((NTP, 256, 256), BF16),
    qall=((512, WIDTH), BF16),
    pick=((SORTED, 512), BF16),
    qs=((SORTED, WIDTH), BF16),
    table=((8, 128), I32),
    new_k=((256, WIDTH), BF16),
    new_v=((256, WIDTH), BF16),
    scores=((256, 2048), F32),
    weights=((256, 2048), BF16),
    leaf_q=((256, WIDTH), BF16),
    leaf_s=((256, WIDTH), F32),
    parts=((512, MSG), BF16),
    arrived=((NREQ, ROWS, MSG), BF16),
    rs_out=((NTP, ROWS, WIDTH), BF16),
    rs_in=((NTP, ROWS, WIDTH), BF16),
    ag=((NTP, ROWS, MSG), BF16),
    ds_out=((NTP, ROWS, WIDTH), BF16),
    ds_in=((NTP, ROWS, WIDTH), BF16),
    proj=((2 * ROWS, 1024), F32),
)


def sized(passes):
    gathered = -(-(SORTED + passes * MID_ROWS) // 128) * 128
    return dict(WORK, back=((512, gathered), BF16), xs=((gathered, MSG), BF16))


def layer_kernel(passes, *refs):
    sizes = sized(passes)
    gathered = sizes["xs"][0][0]
    mid_end = SORTED + passes * MID_ROWS
    small_hbm = refs[:10]
    wq_hbm, wkv_hbm, wout_hbm, wgu_hbm, wdn_hbm, root_hbm, mid_hbm, leaf_hbm, held_hbm = refs[10:19]
    out_ref = refs[19]
    small = refs[20:30]
    v = dict(zip(sizes, refs[30 : 30 + len(sizes)]))
    table_s, copy_sem, hsem, qsem, asem, rsem, gsem, dsem = refs[30 + len(sizes) :]
    stream_v, again_v, mgain_v, lp_v, mp_v, rl_v, ml_v, ll_v, rr_v, freq_v = small
    rank = lax.axis_index("req")
    tp = lax.axis_index("tp")

    def req_peer(d):
        return lax.rem(rank + d, NREQ)

    def tp_peer(d):
        return lax.rem(tp + d, NTP)

    def send(src, dst, sems, d, target):
        copy = pltpu.make_async_remote_copy(
            src_ref=src,
            dst_ref=dst,
            send_sem=sems.at[0, d],
            recv_sem=sems.at[1, d],
            device_id=target,
        )
        copy.start()
        return copy

    barrier = pltpu.get_barrier_semaphore()
    for d in range(1, NREQ):
        pl.semaphore_signal(barrier, inc=1, device_id={"req": req_peer(d)})
    for d in range(1, NTP):
        pl.semaphore_signal(barrier, inc=1, device_id={"tp": tp_peer(d)})

    small_copies = [
        pltpu.make_async_copy(src, dst, copy_sem.at[i])
        for i, (src, dst) in enumerate(zip(small_hbm, small))
    ]
    wq_copy = pltpu.make_async_copy(wq_hbm, v["wq"], copy_sem.at[10])
    wkv_copy = pltpu.make_async_copy(wkv_hbm.reshape(2 * D, WIDTH), v["wkv"], copy_sem.at[11])
    root_copy = pltpu.make_async_copy(root_hbm.reshape(4096, WIDTH), v["root"], copy_sem.at[12])
    mid_copy = pltpu.make_async_copy(mid_hbm.reshape(4096, WIDTH), v["mid"], copy_sem.at[13])
    leaf_copy = pltpu.make_async_copy(leaf_hbm.reshape(8192, WIDTH), v["leaf"], copy_sem.at[14])
    wout_copy = pltpu.make_async_copy(wout_hbm, v["wout"], copy_sem.at[15])
    wgu_copy = pltpu.make_async_copy(wgu_hbm.reshape(2 * D, 1024), v["wgu"], copy_sem.at[16])
    wdn_copy = pltpu.make_async_copy(wdn_hbm, v["wdn"], copy_sem.at[17])
    held_copy = pltpu.make_async_copy(held_hbm.at[0], v["held"].at[tp], copy_sem.at[18])
    for copy in small_copies + [wq_copy, held_copy, wkv_copy, root_copy, mid_copy]:
        copy.start()
    for copy in small_copies:
        copy.wait()
    held_copy.wait()
    pl.semaphore_wait(barrier, NREQ + NTP - 2)
    held_copies = [
        send(v["held"].at[tp], v["held"].at[tp], hsem, d, {"tp": tp_peer(d)}) for d in range(1, NTP)
    ]

    gain = again_v[...].reshape(1, D).astype(F32)
    x = stream_v[...].astype(F32)
    normed = (
        x * lax.rsqrt(jnp.mean(x * x, axis=-1, keepdims=True) + EPSILON) * gain
    ).astype(BF16)
    lp_row = lp_v[...].reshape(1, 512)
    mp_col = as_col(mp_v[...].reshape(1, 16).astype(F32))
    ml_col = as_col(ml_v[...].reshape(1, 16).astype(F32))
    rl_row = rl_v[...].reshape(1, 8).astype(F32)
    parent_len = total(jnp.where(iota((16, 8), 1).astype(F32) == mp_col, rl_row, 0.0), 1)
    belongs = iota((16, 512), 0) == lp_row
    base_row = total(jnp.where(belongs, parent_len + ml_col, 0.0), 0)
    mine = iota((ROWS, 512), 1) == iota((ROWS, 512), 0) + rank * ROWS
    leaf_len_row = ll_v[...].reshape(1, ROWS).astype(F32)
    positions = total(jnp.where(mine, base_row, 0.0), 1) + as_col(leaf_len_row)
    freq = freq_v[...]
    cosines, sines = rope_tables(positions, freq)
    wq_copy.wait()
    queries = rope(dot(normed, v["wq"][...]), cosines, sines).astype(BF16)
    queries = (queries.astype(F32) * (HEAD_DIM**-0.5)).astype(BF16)
    own_rows = pl.ds(pl.multiple_of(rank * ROWS, ROWS), ROWS)
    v["qall"][own_rows, :] = queries
    q_slot = v["qall"].at[own_rows]
    q_copies = [send(q_slot, q_slot, qsem, d, {"req": req_peer(d)}) for d in range(1, NREQ)]
    for copy in (leaf_copy, wout_copy, wgu_copy, wdn_copy):
        copy.start()

    root_row = total(jnp.where(belongs, mp_col, 0.0), 0)
    by_root = (iota((8, 512), 0).astype(F32) == root_row).astype(F32)
    in_mid = lp_row == rank
    groups = jnp.concatenate(
        [by_root, jnp.broadcast_to(in_mid.astype(F32), (8, 512))], axis=0
    ).astype(BF16)
    before = (iota((512, 512), 0) < iota((512, 512), 1)).astype(BF16)
    order = dot(groups, before)
    blocks = jnp.floor((total(by_root, 1) + (BLOCK - 1)) * (1.0 / BLOCK))
    first = total(jnp.where(iota((8, 8), 1) < iota((8, 8), 0), as_row(blocks), 0.0), 1)
    dest = total(by_root * (order[:8] + first * BLOCK), 0)
    ends = (first + blocks) <= iota((8, 128), 1).astype(F32)
    root_of = jnp.minimum(total(ends.astype(F32), 0), 7.0)
    v["table"][...] = jnp.broadcast_to(root_of, (8, 128)).astype(I32)
    table_copy = pltpu.make_async_copy(v["table"], table_s, copy_sem.at[19])
    table_copy.start()
    mid_order = order[8:9]
    v["pick"][...] = (iota((SORTED, 512), 0) == dest.astype(I32)).astype(BF16)
    final = as_col(jnp.where(in_mid, SORTED + mid_order, dest)).astype(I32)
    v["back"][...] = (iota((512, gathered), 1) == final).astype(BF16)
    if gathered > mid_end:
        v["xs"][mid_end:, :] = jnp.zeros((gathered - mid_end, MSG), BF16)
    lane256 = iota((1, 256), 1)
    for r in range(8):
        v["root_bias"][r] = jnp.where(
            (lane256 + rank * 256).astype(F32) < rl_row[:, r : r + 1], 0.0, NEG_FILL
        )
    own_len = total(jnp.where(iota((16, 1), 0) == rank, ml_col, 0.0), 0)
    own_parent = total(jnp.where(iota((16, 1), 0) == rank, parent_len, 0.0), 0)
    rr = rr_v[...]
    rr_col = as_col(rr.astype(F32))
    slot_col = rr_col.astype(I32)
    hit_hi = (iota((16, 256), 0) == rr // 128).astype(BF16)
    hit_lo = (iota((256, 128), 1) == slot_col % 128).astype(BF16)
    token = (iota((16, 128), 0) * 128 + iota((16, 128), 1)).astype(F32)
    alive = (token < own_len) & (dot(hit_hi, hit_lo) < 0.5)
    v["mid_bias"][...] = jnp.where(alive, 0.0, NEG_FILL)
    new_bias = jnp.where(rr.astype(F32) < own_len, 0.0, NEG_FILL)
    held_cos, held_sin = rope_tables(own_parent + rr_col, freq)

    r2, c2 = iota((256, 256), 0), iota((256, 256), 1)
    split = (c2 == jnp.where(r2 < 128, 2 * r2, 2 * r2 - 255)).astype(BF16)
    wkv_copy.wait()
    split_pairs(split, v["wkv"], v["wk"], v["wv"], 16)
    root_copy.wait()
    for k in range(16):
        both = dot(split, v["root"][k * 256 : (k + 1) * 256, :]).astype(BF16)
        half = slice((k % 2) * 128, (k % 2) * 128 + 128)
        v["root_k"][k // 2, half, :] = both[:128]
        v["root_v"][k // 2, half, :] = both[128:]
    mid_copy.wait()
    split_pairs(split, v["mid"], v["mid_k"], v["mid_v"], 16)
    key_new = rope(dot(normed, v["wk"][...]), cosines, sines).astype(BF16)
    value_new = dot(normed, v["wv"][...]).astype(BF16)

    for copy in q_copies:
        copy.wait_recv()
    v["qs"][...] = dot(v["pick"][...], v["qall"][...]).astype(BF16)
    block_mask = (iota((128, WIDTH), 0) // BLOCK == iota((128, WIDTH), 1) // HEAD_DIM).astype(BF16)
    table_copy.wait()

    def root_block(j):
        at = pl.ds(pl.multiple_of(j * BLOCK, BLOCK), BLOCK)
        q = v["qs"][at, :]
        qbd = jnp.concatenate([q] * HEADS, axis=0) * block_mask
        root = jnp.clip(table_s[0, j], 0, 7)
        scores = dot_t(qbd, v["root_k"][root]) + v["root_bias"][root]
        m = jnp.max(scores, axis=1, keepdims=True)
        weights = jnp.exp(scores - m)
        row_sum = total(weights, 1)
        acc = dot(weights.astype(BF16), v["root_v"][root])
        out = head_columns(acc, BLOCK, WIDTH) / head_columns(row_sum, BLOCK, WIDTH)
        lse = head_columns(m + jnp.log(row_sum), BLOCK, STATS)
        v["xs"][at, :] = packed(out, lse)

    def root_blocks(i, carry):
        for u in range(4):
            root_block(i * 4 + u)
        return carry

    lax.fori_loop(0, BLOCKS // 4, root_blocks, 0)

    for copy in held_copies:
        copy.wait_recv()
    square = jnp.zeros((256, 1), F32)
    for c in range(NTP):
        part = v["held"][c].astype(F32)
        square = square + total(part * part, 1)
    scale = lax.rsqrt(square * (1.0 / D) + EPSILON)
    keys = jnp.zeros((256, WIDTH), F32)
    values = jnp.zeros((256, WIDTH), F32)
    for c in range(NTP):
        rows = slice(c * 256, (c + 1) * 256)
        part = (v["held"][c].astype(F32) * scale * gain[:, rows]).astype(BF16)
        keys = keys + dot(part, v["wk"][rows, :])
        values = values + dot(part, v["wv"][rows, :])
    v["new_k"][...] = rope(keys, held_cos, held_sin).astype(BF16)
    v["new_v"][...] = values.astype(BF16)

    mid_mask = (iota((256, WIDTH), 0) // MID_ROWS == iota((256, WIDTH), 1) // HEAD_DIM).astype(BF16)
    e0, e1 = iota((STATS, WIDTH), 0), iota((STATS, WIDTH), 1)
    expand3 = ((e0 < 12) & ((e0 % HEADS) == e1 // HEAD_DIM)).astype(BF16)
    expand2 = ((e0 < 8) & ((e0 % HEADS) == e1 // HEAD_DIM)).astype(BF16)
    lane64 = iota((MID_ROWS, STATS), 1)

    def mid_pass(p):
        chosen = (iota((MID_ROWS, 512), 0) + p * MID_ROWS == mid_order.astype(I32)) & in_mid
        mid_dest = total(jnp.where(chosen, dest, 0.0), 1)
        q_mid = dot(chosen.astype(BF16), v["qall"][...]).astype(BF16)
        take = (iota((MID_ROWS, SORTED), 1) == mid_dest.astype(I32)).astype(BF16)
        rooted = dot(take, v["xs"][:SORTED, :])
        qbd = jnp.concatenate([q_mid] * HEADS, axis=0) * mid_mask
        fresh = dot_t(qbd, v["new_k"][...]) + new_bias
        m = jnp.max(fresh, axis=1, keepdims=True)
        for c in range(8):
            cols = slice(c * 256, (c + 1) * 256)
            bias = jnp.concatenate(
                [v["mid_bias"][2 * c : 2 * c + 1, :], v["mid_bias"][2 * c + 1 : 2 * c + 2, :]], axis=1
            )
            scores = dot_t(qbd, v["mid_k"][cols, :]) + bias
            v["scores"][:, cols] = scores
            m = jnp.maximum(m, jnp.max(scores, axis=1, keepdims=True))
        weights = jnp.exp(fresh - m)
        row_sum = total(weights, 1)
        acc = dot(weights.astype(BF16), v["new_v"][...])
        for c in range(8):
            cols = slice(c * 256, (c + 1) * 256)
            weights = jnp.exp(v["scores"][:, cols] - m)
            row_sum = row_sum + total(weights, 1)
            v["weights"][:, cols] = weights.astype(BF16)
        acc = acc + dot(v["weights"][...], v["mid_v"][...])
        mid_out = head_columns(acc, MID_ROWS, WIDTH) / head_columns(row_sum, MID_ROWS, WIDTH)
        mid_lse = m + jnp.log(row_sum)
        lse_a = dot(rooted[:, WIDTH:].astype(BF16), expand3)
        lse_b = head_columns(mid_lse, MID_ROWS, WIDTH)
        top = jnp.maximum(lse_a, lse_b)
        part_a, part_b = jnp.exp(lse_a - top), jnp.exp(lse_b - top)
        merged = (part_a * rooted[:, :WIDTH] + part_b * mid_out) / (part_a + part_b)
        lse_a = jnp.where(lane64 < 4, unpacked_lse(rooted[:, WIDTH:]), 0.0)
        lse_a = lse_a + pltpu.roll(lse_a, 4, 1) + pltpu.roll(lse_a, 8, 1)
        lse_b = head_columns(mid_lse, MID_ROWS, STATS)
        top = jnp.maximum(lse_a, lse_b)
        joined = top + jnp.log(jnp.exp(lse_a - top) + jnp.exp(lse_b - top))
        at = SORTED if passes == 1 else pl.multiple_of(SORTED + p * MID_ROWS, MID_ROWS)
        v["xs"][pl.ds(at, MID_ROWS), :] = packed(merged, joined)

    if passes == 1:
        mid_pass(0)
    else:

        def mid_step(p, carry):
            mid_pass(p)
            return carry

        lax.fori_loop(0, passes, mid_step, 0)

    v["parts"][...] = dot(v["back"][...], v["xs"][...]).astype(BF16)
    a_copies = []
    for d in range(1, NREQ):
        peer = req_peer(d)
        rows = pl.ds(pl.multiple_of(peer * ROWS, ROWS), ROWS)
        a_copies.append(
            send(v["parts"].at[rows], v["arrived"].at[d], asem, d, {"req": peer})
        )
    v["arrived"][0] = v["parts"][own_rows, :]

    repeat = (iota((256, ROWS), 0) // 8 == iota((256, ROWS), 1)).astype(BF16)
    head_mask = (r2 % 8) == (c2 // HEAD_DIM)
    qrep = jnp.where(head_mask, dot(repeat, queries), 0.0)
    v["leaf_q"][...] = qrep.astype(BF16)
    self_score = total(qrep * dot(repeat, key_new), 1)
    live_len = total(repeat.astype(F32) * leaf_len_row, 1)
    leaf_copy.wait()
    for r in range(ROWS):
        v["leaf_s"][r * 8 : (r + 1) * 8, :] = dot_t(
            v["leaf_q"][r * 8 : (r + 1) * 8, :], v["leaf"][r * 256 : (r + 1) * 256, :]
        )
    live = ((c2 % 2) == 1) & ((c2 // 2).astype(F32) < live_len)
    scores = jnp.where(live, shift_pairs(v["leaf_s"][...]), NEG_FILL)
    best = jnp.maximum(jnp.max(scores, axis=1, keepdims=True), self_score)
    weights = jnp.exp(scores - best)
    self_weight = jnp.exp(self_score - best)
    row_sum = total(weights, 1) + self_weight
    v["leaf_q"][...] = weights.astype(BF16)
    for r in range(ROWS):
        v["leaf_s"][r * 8 : (r + 1) * 8, :] = dot(
            v["leaf_q"][r * 8 : (r + 1) * 8, :], v["leaf"][r * 256 : (r + 1) * 256, :]
        )
    acc = v["leaf_s"][...] + self_weight.astype(BF16).astype(F32) * dot(repeat, value_new)
    acc = jnp.where(head_mask, acc / row_sum, 0.0)
    leaf_out = jnp.sum(acc.reshape(ROWS, 8, WIDTH), axis=1)
    lse = best + jnp.log(row_sum)
    spread = jnp.where((r2 % 8)[:, :STATS] == c2[:, :STATS], lse, 0.0)
    leaf_lse = jnp.sum(spread.reshape(ROWS, 8, STATS), axis=1)

    lane = iota((ROWS, STATS), 1)
    for copy in a_copies:
        copy.wait_recv()
    lses = [unpacked_lse(v["arrived"][s, :, WIDTH:].astype(F32)) for s in range(NREQ)]
    lses.append(leaf_lse)
    best = lses[0]
    for value in lses[1:]:
        best = jnp.maximum(best, value)
    shares = [jnp.exp(value - best) for value in lses]
    row_sum = shares[0]
    for value in shares[1:]:
        row_sum = row_sum + value
    attended = jnp.zeros((ROWS, WIDTH), F32)
    for s in range(NREQ + 1):
        share = shares[s] / row_sum
        high = share.astype(BF16).astype(F32)
        both = jnp.where(
            lane < 4, high, jnp.where(lane < 8, pltpu.roll(share - high, 4, 1), 0.0)
        )
        factor = dot(both.astype(BF16), expand2)
        source = v["arrived"][s, :, :WIDTH].astype(F32) if s < NREQ else leaf_out
        attended = attended + factor * source
    attended = attended.astype(BF16)

    own_cols = pl.ds(pl.multiple_of(tp * WIDTH, WIDTH), WIDTH)

    def scatter(left, weight_v, outgoing, incoming, sems):
        copies = []
        for d in range(1, NTP):
            peer = tp_peer(d)
            cols = pl.ds(pl.multiple_of(peer * WIDTH, WIDTH), WIDTH)
            outgoing[d] = dot(left, weight_v[:, cols]).astype(BF16)
            copies.append(send(outgoing.at[d], incoming.at[d], sems, d, {"tp": peer}))
        return copies, dot(left, weight_v[:, own_cols])

    wout_copy.wait()
    r_copies, own_part = scatter(attended, v["wout"], v["rs_out"], v["rs_in"], rsem)
    residual = own_part + stream_v[:, own_cols].astype(F32)
    i2, j2 = iota((256, 512), 0), iota((256, 512), 1)
    to_even = (j2 == 2 * i2).astype(BF16)
    to_odd = (j2 == 2 * i2 + 1).astype(BF16)
    gain_row = mgain_v[...].reshape(1, D).astype(F32)
    own_gain = jnp.zeros((1, WIDTH), F32)
    for c in range(NTP):
        own_gain = jnp.where(tp == c, gain_row[:, c * WIDTH : (c + 1) * WIDTH], own_gain)
    for d in range(1, NTP):
        r_copies[d - 1].wait_recv()
        residual = residual + v["rs_in"][d].astype(F32)

    a, b, c = three_terms(jnp.broadcast_to(total(residual * residual, 1), (ROWS, STATS)))
    stats = jnp.where(
        lane == 0,
        a.astype(F32),
        jnp.where(lane == 1, b.astype(F32), jnp.where(lane == 2, c.astype(F32), 0.0)),
    )
    v["ag"][0] = jnp.concatenate([residual * own_gain, stats], axis=1).astype(BF16)
    g_copies = [
        send(v["ag"].at[0], v["ag"].at[d], gsem, d, {"tp": tp_peer(d)}) for d in range(1, NTP)
    ]
    wgu_copy.wait()
    squares = jnp.zeros((ROWS, STATS), F32)
    for d in range(NTP):
        if d > 0:
            g_copies[d - 1].wait_recv()
        owner = tp_peer(NTP - d)
        part = v["ag"][d]
        squares = squares + part[:, WIDTH:].astype(F32)
        chunk = part[:, :WIDTH]
        mixed = jnp.concatenate([dot(chunk, to_even), dot(chunk, to_odd)], axis=0).astype(BF16)
        rows = pl.ds(pl.multiple_of(owner * 512, 512), 512)
        for n in range(4):
            cols = slice(n * 256, (n + 1) * 256)
            product = dot(mixed, v["wgu"][rows, cols])
            if d == 0:
                v["proj"][:, cols] = product
            else:
                v["proj"][:, cols] += product
    scale = lax.rsqrt(total(squares, 1) * (1.0 / D) + EPSILON)
    gate = v["proj"][:ROWS, :] * scale
    up = v["proj"][ROWS:, :] * scale
    hidden = (gate / (1.0 + jnp.exp(-gate)) * up).astype(BF16)
    wdn_copy.wait()
    d_copies, own_part = scatter(hidden, v["wdn"], v["ds_out"], v["ds_in"], dsem)
    result = residual + own_part
    for d in range(1, NTP):
        d_copies[d - 1].wait_recv()
        result = result + v["ds_in"][d].astype(F32)
    out_ref[...] = result.astype(BF16)
    for copy in held_copies + q_copies + a_copies + r_copies + g_copies + d_copies:
        copy.wait_send()


def layer_device(
    passes,
    stream,
    attn_gain,
    mlp_gain,
    w_query,
    w_keyval,
    w_out,
    w_gate_up,
    w_down,
    root_cache,
    mid_cache,
    leaf_cache,
    held_hidden,
    recompute_rows,
    root_len,
    mid_len,
    leaf_len,
    mid_parent,
    leaf_parent,
):
    freq = np.exp(np.arange(32, dtype=np.float32) * np.float32(-2.0 * math.log(THETA_BASE) / HEAD_DIM))
    freq = jnp.asarray(np.tile(freq.astype(np.float32), 4)[None, :])
    dma = pltpu.SemaphoreType.DMA
    return pl.pallas_call(
        functools.partial(layer_kernel, passes),
        name="layer" if passes == 1 else "layer_crowded",
        out_shape=jax.ShapeDtypeStruct((ROWS, WIDTH), BF16),
        in_specs=[pl.BlockSpec(memory_space=pltpu.HBM)] * 19,
        out_specs=pl.BlockSpec(memory_space=pltpu.VMEM),
        scratch_shapes=[pltpu.VMEM(*s) for s in SMALL]
        + [pltpu.VMEM(*s) for s in sized(passes).values()]
        + [
            pltpu.SMEM((8, 128), I32),
            dma((20,)),
            dma((2, NTP)),
            dma((2, NREQ)),
            dma((2, NREQ)),
            dma((2, NTP)),
            dma((2, NTP)),
            dma((2, NTP)),
        ],
        compiler_params=pltpu.CompilerParams(
            collective_id=0 if passes == 1 else 1, has_side_effects=True, vmem_limit_bytes=56 * 1024 * 1024
        ),
    )(
        stream,
        attn_gain,
        mlp_gain,
        leaf_parent,
        mid_parent,
        root_len,
        mid_len,
        leaf_len,
        recompute_rows,
        freq,
        w_query,
        w_keyval,
        w_out,
        w_gate_up,
        w_down,
        root_cache,
        mid_cache,
        leaf_cache,
        held_hidden,
    )


def on_device(*args):
    leaf_parent = args[17]
    counts = jnp.sum(
        (leaf_parent[None, :] == jnp.arange(16, dtype=I32)[:, None]).astype(I32), axis=1
    )
    usual = functools.partial(layer_device, 1)
    crowded = functools.partial(layer_device, 512 // MID_ROWS)
    return lax.cond(jnp.max(counts) <= MID_ROWS, usual, crowded, *args)


def solution(mesh):
    placed = (
        P("req", None),
        P(),
        P(),
        P(None, "tp"),
        P(None, None, "tp"),
        P("tp", None),
        P(None, None, "tp"),
        P("tp", None),
        P(None, "req", None, "tp"),
        P("req", None, None, "tp"),
        P("req", None, None, "tp"),
        P("req", None, "tp"),
        P("req", None),
        P(),
        P(),
        P("req"),
        P(),
        P(),
    )
    return jax.shard_map(
        on_device, mesh=mesh, in_specs=placed, out_specs=P("req", "tp"), check_vma=False
    )
```

time: 372 us -> 52.7 us (0.14); the launches traced: 367 us -> 52.5 us
  local copies, waits for them, and re-layouts: 124 us -> 0.61 us
  waiting for transfers between devices: 78.1 us -> 0 us
  blocking collectives: 57.3 us -> 0 us
  Pallas kernels: 0 us -> 49.3 us
  other arithmetic: 50 us -> 1.44 us
  matrix products: 44.2 us -> 0 us
  between operations: 13.6 us -> 0.66 us
    all_gather x3 -> x0, blocking collectives: 57.3 us -> none  [the longest x2 37.4 us: combined_all(): everything = jax.tree.map(lambda part: lax.all_gather(part, axis), value)]
    pallas_call x0 -> x1, Pallas kernels: none -> 49.3 us  [layer_device(): pl.pallas_call(functools.partial(layer_kernel, passes), name='layer' if p...]
    unnamed x53 -> x1, local copies, waits for them, and re-layouts: 49.1 us -> 0.61 us
    dot_general x12 -> x0, matrix products: 44.2 us -> none  [the longest x2 14.8 us: partial_softmax(): jnp.einsum('hbk,khd->bhd', weights.astype(jnp.bfloat16), value_part, pref...]
    psum x1 -> x0, waiting for transfers between devices: 40.9 us -> none  [on_device(): residual = stream_float + lax.psum(attn_part, 'tp')]
    slice x9 -> x0, local copies, waits for them, and re-layouts: 31.2 us -> none  [the longest x3 15 us: partial_softmax(): value_part = key_rows[:, 1].reshape(count, heads, HEAD_DIM)]
    reduce_scatter x1 -> x0, waiting for transfers between devices: 29 us -> none  [on_device(): lax.psum_scatter(jnp.dot(hidden, w_down, preferred_element_type=jnp.float...]
    dynamic_slice x35 -> x0, local copies, waits for them, and re-layouts: 22.6 us -> none  [the longest x30 19.2 us: lap(): return combine(so_far, jax.tree.map(lambda part: part[k], everything))]
  transfers between devices with their start and end apart: 4 -> 0, of which waited for: 3 -> 0; matrix products, arithmetic and copies ran while one was open for 31% -> 0% of each run, Pallas kernels for 0% -> 0%
where the time goes in v2:
time: 52.7 us; the launch traced here: 52.5 us
  Pallas kernels  49.3 us (94%)
  other arithmetic  1.44 us (3%)
  between operations  0.66 us (1%)
  local copies, waits for them, and re-layouts  0.61 us (1%)
  loops' own time  0.54 us (1%)
    pallas_call x1, Pallas kernels, layer_device(): pl.pallas_call(functools.partial(layer_kernel, passes), name='layer' if p...  49.3 us

profile of v2, /device:TPU:1, one launch (start us, length us, event | category | flops | bytes accessed | tf_op | source)
XLA Modules:
  0.0 52.5 jit_solution(6536326870932818785)
XLA Ops:
  0.0 0.8 %convert_reduce_fusion = s32[16]{0:T(128)S(1)} fusion(s32[512]{0:T(512)} %param.39), kind=kLoop, calls=%fused_computation | loop fusion | flops 24560 | bytes 2112 | tf_op jit(solution)/shard_map/reduce_sum | solution.py:623
  0.8 0.6 %reduce_max.9 = s32[]{:T(128)} reduce(s32[16]{0:T(128)S(1)} %convert_reduce_fusion, s32[]{:T(128)} %constant.2.clone.1), dimensions={0}, to_apply=%region_1.0 | reduce | flops 15 | bytes 72 | tf_op jit(solution)/shard_map/reduce_max | solution.py:628
  2.1 49.8 %conditional.1 = (bf16[32,256]{1,0:T(8,128)(2,1)S(1)}) conditional(s32[]{:T(128)} %convert_element_type.7, (bf16[32,2048]{1,0:T(8,128)(2,1)}, bf16[2048]{0:T(1024)(128)(2,1)}, bf16[2048]{0:T(1024)(128)(2,1)}, s32[512]{0:T(512)}, s32[16]{0:T(128)}, /*index=5*/s32[8]{0:T(128)}, s32[16]{0:T(128)}, s32[32]{0:T(128)}, s32[1,256]{1,0:T(1,128)}, ...), branch_computations={%region_2.0_spmd, %region_3.0_spmd} | conditional | bytes 8 | solution.py:628
  2.3 49.3 %layer.1 = bf16[32,256]{1,0:T(8,128)(2,1)S(1)} custom-call(bf16[32,2048]{1,0:T(8,128)(2,1)} %get-tuple-element.103.refs_0_, bf16[2048]{0:T(1024)(128)(2,1)} %get-tuple-element.104.refs_1_, bf16[2048]{0:T(1024)(128)(2,1)} %get-tuple-element.105.refs_2_, s32[512]{0:T(512)} %get-tuple-element.106.refs_3_, s32[16]{0:T(128)} %get-tuple-element.107.refs_4_, ...), custom_call_target="tpu_custom_call" | custom-call | tf_op jit(solution)/shard_map/cond/branch_1_fun/layer/pallas_call | solution.py:577
  51.9 0.6 %copy.26 = bf16[32,256]{1,0:T(8,128)(2,1)} copy(bf16[32,256]{1,0:T(8,128)(2,1)S(1)} %get-tuple-element.122) | data formatting | bytes 32768

commit v3 on v2

--- a/solution.py
+++ b/solution.py
@@ -24,6 +24,7 @@
 HEADS = 4
 BLOCK = 32
 BLOCKS = 24
+GROUP = 8
 SORTED = BLOCKS * BLOCK
 MID_ROWS = 64
 STATS = 128
@@ -164,7 +165,8 @@
     arrived=((NREQ, ROWS, MSG), BF16),
     rs_out=((NTP, ROWS, WIDTH), BF16),
     rs_in=((NTP, ROWS, WIDTH), BF16),
-    ag=((NTP, ROWS, MSG), BF16),
+    ag=((NTP, ROWS, WIDTH), BF16),
+    gain=((1, D), F32),
     ds_out=((NTP, ROWS, WIDTH), BF16),
     ds_in=((NTP, ROWS, WIDTH), BF16),
     proj=((2 * ROWS, 1024), F32),
@@ -230,11 +232,6 @@
         copy.start()
     for copy in small_copies:
         copy.wait()
-    held_copy.wait()
-    pl.semaphore_wait(barrier, NREQ + NTP - 2)
-    held_copies = [
-        send(v["held"].at[tp], v["held"].at[tp], hsem, d, {"tp": tp_peer(d)}) for d in range(1, NTP)
-    ]
 
     gain = again_v[...].reshape(1, D).astype(F32)
     x = stream_v[...].astype(F32)
@@ -256,6 +253,17 @@
     wq_copy.wait()
     queries = rope(dot(normed, v["wq"][...]), cosines, sines).astype(BF16)
     queries = (queries.astype(F32) * (HEAD_DIM**-0.5)).astype(BF16)
+    held_copy.wait()
+    pl.semaphore_wait(barrier, NREQ + NTP - 2)
+
+    after, ahead, across, sibling = tp_peer(2), tp_peer(6), tp_peer(4), tp + 1 - 2 * lax.rem(tp, 2)
+    held = v["held"]
+    low, high = slice(0, 128), slice(128, 256)
+    held_copies = [
+        send(held.at[tp], held.at[tp], hsem, 0, {"tp": after}),
+        send(held.at[tp], held.at[tp], hsem, 1, {"tp": ahead}),
+        send(held.at[tp], held.at[tp], hsem, 4, {"tp": sibling}),
+    ]
     own_rows = pl.ds(pl.multiple_of(rank * ROWS, ROWS), ROWS)
     v["qall"][own_rows, :] = queries
     q_slot = v["qall"].at[own_rows]
@@ -313,6 +321,15 @@
         half = slice((k % 2) * 128, (k % 2) * 128 + 128)
         v["root_k"][k // 2, half, :] = both[:128]
         v["root_v"][k // 2, half, :] = both[128:]
+    held_copies[0].wait_recv()
+    held_copies[1].wait_recv()
+    held_copies += [
+        send(held.at[ahead, low], held.at[ahead, low], hsem, 2, {"tp": after}),
+        send(held.at[after, high], held.at[after, high], hsem, 3, {"tp": ahead}),
+        send(held.at[ahead], held.at[ahead], hsem, 5, {"tp": sibling}),
+        send(held.at[after], held.at[after], hsem, 6, {"tp": sibling}),
+    ]
+
     mid_copy.wait()
     split_pairs(split, v["mid"], v["mid_k"], v["mid_v"], 16)
     key_new = rope(dot(normed, v["wk"][...]), cosines, sines).astype(BF16)
@@ -321,31 +338,41 @@
     for copy in q_copies:
         copy.wait_recv()
     v["qs"][...] = dot(v["pick"][...], v["qall"][...]).astype(BF16)
+    held_copies[3].wait_recv()
+    held_copies[4].wait_recv()
+    held_copies += [
+        send(held.at[across, low], held.at[across, low], hsem, 7, {"tp": sibling}),
+        send(held.at[across, high], held.at[across, high], hsem, 8, {"tp": sibling}),
+    ]
     block_mask = (iota((128, WIDTH), 0) // BLOCK == iota((128, WIDTH), 1) // HEAD_DIM).astype(BF16)
     table_copy.wait()
 
-    def root_block(j):
-        at = pl.ds(pl.multiple_of(j * BLOCK, BLOCK), BLOCK)
-        q = v["qs"][at, :]
-        qbd = jnp.concatenate([q] * HEADS, axis=0) * block_mask
-        root = jnp.clip(table_s[0, j], 0, 7)
-        scores = dot_t(qbd, v["root_k"][root]) + v["root_bias"][root]
-        m = jnp.max(scores, axis=1, keepdims=True)
-        weights = jnp.exp(scores - m)
-        row_sum = total(weights, 1)
-        acc = dot(weights.astype(BF16), v["root_v"][root])
-        out = head_columns(acc, BLOCK, WIDTH) / head_columns(row_sum, BLOCK, WIDTH)
-        lse = head_columns(m + jnp.log(row_sum), BLOCK, STATS)
-        v["xs"][at, :] = packed(out, lse)
-
     def root_blocks(i, carry):
-        for u in range(4):
-            root_block(i * 4 + u)
+        ats = [
+            pl.ds(pl.multiple_of((i * GROUP + u) * BLOCK, BLOCK), BLOCK) for u in range(GROUP)
+        ]
+        roots = [jnp.clip(table_s[0, i * GROUP + u], 0, 7) for u in range(GROUP)]
+        qbds = [jnp.concatenate([v["qs"][at, :]] * HEADS, axis=0) * block_mask for at in ats]
+        scores = [
+            dot_t(qbd, v["root_k"][root]) + v["root_bias"][root] for qbd, root in zip(qbds, roots)
+        ]
+        tops = [jnp.max(score, axis=1, keepdims=True) for score in scores]
+        weights = [jnp.exp(score - m) for score, m in zip(scores, tops)]
+        sums = [total(weight, 1) for weight in weights]
+        accs = [
+            dot(weight.astype(BF16), v["root_v"][root]) for weight, root in zip(weights, roots)
+        ]
+        outs = []
+        for m, row_sum, acc in zip(tops, sums, accs):
+            out = head_columns(acc, BLOCK, WIDTH) / head_columns(row_sum, BLOCK, WIDTH)
+            outs.append(packed(out, head_columns(m + jnp.log(row_sum), BLOCK, STATS)))
+        for at, out in zip(ats, outs):
+            v["xs"][at, :] = out
         return carry
 
-    lax.fori_loop(0, BLOCKS // 4, root_blocks, 0)
-
-    for copy in held_copies:
+    lax.fori_loop(0, BLOCKS // GROUP, root_blocks, 0)
+
+    for copy in [held_copies[2]] + held_copies[5:]:
         copy.wait_recv()
     square = jnp.zeros((256, 1), F32)
     for c in range(NTP):
@@ -500,32 +527,25 @@
     to_even = (j2 == 2 * i2).astype(BF16)
     to_odd = (j2 == 2 * i2 + 1).astype(BF16)
     gain_row = mgain_v[...].reshape(1, D).astype(F32)
-    own_gain = jnp.zeros((1, WIDTH), F32)
-    for c in range(NTP):
-        own_gain = jnp.where(tp == c, gain_row[:, c * WIDTH : (c + 1) * WIDTH], own_gain)
+    v["gain"][...] = gain_row
     for d in range(1, NTP):
         r_copies[d - 1].wait_recv()
         residual = residual + v["rs_in"][d].astype(F32)
 
-    a, b, c = three_terms(jnp.broadcast_to(total(residual * residual, 1), (ROWS, STATS)))
-    stats = jnp.where(
-        lane == 0,
-        a.astype(F32),
-        jnp.where(lane == 1, b.astype(F32), jnp.where(lane == 2, c.astype(F32), 0.0)),
-    )
-    v["ag"][0] = jnp.concatenate([residual * own_gain, stats], axis=1).astype(BF16)
+    v["ag"][0] = residual.astype(BF16)
     g_copies = [
         send(v["ag"].at[0], v["ag"].at[d], gsem, d, {"tp": tp_peer(d)}) for d in range(1, NTP)
     ]
     wgu_copy.wait()
-    squares = jnp.zeros((ROWS, STATS), F32)
+    squares = jnp.zeros((ROWS, WIDTH), F32)
     for d in range(NTP):
         if d > 0:
             g_copies[d - 1].wait_recv()
         owner = tp_peer(NTP - d)
-        part = v["ag"][d]
-        squares = squares + part[:, WIDTH:].astype(F32)
-        chunk = part[:, :WIDTH]
+        part = v["ag"][d].astype(F32)
+        squares = squares + part * part
+        gain_cols = pl.ds(pl.multiple_of(owner * WIDTH, WIDTH), WIDTH)
+        chunk = (part * v["gain"][:, gain_cols]).astype(BF16)
         mixed = jnp.concatenate([dot(chunk, to_even), dot(chunk, to_odd)], axis=0).astype(BF16)
         rows = pl.ds(pl.multiple_of(owner * 512, 512), 512)
         for n in range(4):
@@ -585,7 +605,7 @@
         + [
             pltpu.SMEM((8, 128), I32),
             dma((20,)),
-            dma((2, NTP)),
+            dma((2, 9)),
             dma((2, NREQ)),
             dma((2, NREQ)),
             dma((2, NTP)),

time: 52.7 us -> 48.1 us (0.913)
  Pallas kernels: 49.3 us -> 44.7 us
    pallas_call x1, Pallas kernels: 49.3 us -> 44.7 us  [layer_device(): pl.pallas_call(functools.partial(layer_kernel, passes), name='layer' if p...]
where the time goes in v3:
time: 48.1 us; the launch traced here: 47.9 us
  Pallas kernels  44.7 us (93%)
  other arithmetic  1.44 us (3%)
  between operations  0.66 us (1%)
  local copies, waits for them, and re-layouts  0.61 us (1%)
  loops' own time  0.54 us (1%)
    pallas_call x1, Pallas kernels, layer_device(): pl.pallas_call(functools.partial(layer_kernel, passes), name='layer' if p...  44.7 us

profile of v3, /device:TPU:1, one launch (start us, length us, event | category | flops | bytes accessed | tf_op | source)
XLA Modules:
  0.0 47.9 jit_solution(8941857783042300895)
XLA Ops:
  0.0 0.8 %convert_reduce_fusion = s32[16]{0:T(128)S(1)} fusion(s32[512]{0:T(512)} %param.39), kind=kLoop, calls=%fused_computation | loop fusion | flops 24560 | bytes 2112 | tf_op jit(solution)/shard_map/reduce_sum | solution.py:643
  0.8 0.6 %reduce_max.9 = s32[]{:T(128)} reduce(s32[16]{0:T(128)S(1)} %convert_reduce_fusion, s32[]{:T(128)} %constant.2.clone.1), dimensions={0}, to_apply=%region_1.0 | reduce | flops 15 | bytes 72 | tf_op jit(solution)/shard_map/reduce_max | solution.py:648
  2.1 45.2 %conditional.1 = (bf16[32,256]{1,0:T(8,128)(2,1)S(1)}) conditional(s32[]{:T(128)} %convert_element_type.7, (bf16[32,2048]{1,0:T(8,128)(2,1)}, bf16[2048]{0:T(1024)(128)(2,1)}, bf16[2048]{0:T(1024)(128)(2,1)}, s32[512]{0:T(512)}, s32[16]{0:T(128)}, /*index=5*/s32[8]{0:T(128)}, s32[16]{0:T(128)}, s32[32]{0:T(128)}, s32[1,256]{1,0:T(1,128)}, ...), branch_computations={%region_2.0_spmd, %region_3.0_spmd} | conditional | bytes 8 | solution.py:648
  2.3 44.7 %layer.1 = bf16[32,256]{1,0:T(8,128)(2,1)S(1)} custom-call(bf16[32,2048]{1,0:T(8,128)(2,1)} %get-tuple-element.103.refs_0_, bf16[2048]{0:T(1024)(128)(2,1)} %get-tuple-element.104.refs_1_, bf16[2048]{0:T(1024)(128)(2,1)} %get-tuple-element.105.refs_2_, s32[512]{0:T(512)} %get-tuple-element.106.refs_3_, s32[16]{0:T(128)} %get-tuple-element.107.refs_4_, ...), custom_call_target="tpu_custom_call" | custom-call | tf_op jit(solution)/shard_map/cond/branch_1_fun/layer/pallas_call | solution.py:597
  47.3 0.6 %copy.26 = bf16[32,256]{1,0:T(8,128)(2,1)} copy(bf16[32,256]{1,0:T(8,128)(2,1)S(1)} %get-tuple-element.122) | data formatting | bytes 32768

commit v4 on v3

--- a/solution.py
+++ b/solution.py
@@ -161,8 +161,8 @@
     weights=((256, 2048), BF16),
     leaf_q=((256, WIDTH), BF16),
     leaf_s=((256, WIDTH), F32),
-    parts=((512, MSG), BF16),
-    arrived=((NREQ, ROWS, MSG), BF16),
+    parts=((NREQ, ROWS + 8, WIDTH), BF16),
+    arrived=((NREQ, ROWS + 8, WIDTH), BF16),
     rs_out=((NTP, ROWS, WIDTH), BF16),
     rs_in=((NTP, ROWS, WIDTH), BF16),
     ag=((NTP, ROWS, WIDTH), BF16),
@@ -289,7 +289,8 @@
     table_copy.start()
     mid_order = order[8:9]
     v["pick"][...] = (iota((SORTED, 512), 0) == dest.astype(I32)).astype(BF16)
-    final = as_col(jnp.where(in_mid, SORTED + mid_order, dest)).astype(I32)
+    turned = iota((512, 512), 1) == lax.rem(iota((512, 512), 0) + rank * ROWS, 512)
+    final = total(jnp.where(turned, jnp.where(in_mid, SORTED + mid_order, dest), 0.0), 1).astype(I32)
     v["back"][...] = (iota((512, gathered), 1) == final).astype(BF16)
     if gathered > mid_end:
         v["xs"][mid_end:, :] = jnp.zeros((gathered - mid_end, MSG), BF16)
@@ -392,7 +393,6 @@
     mid_mask = (iota((256, WIDTH), 0) // MID_ROWS == iota((256, WIDTH), 1) // HEAD_DIM).astype(BF16)
     e0, e1 = iota((STATS, WIDTH), 0), iota((STATS, WIDTH), 1)
     expand3 = ((e0 < 12) & ((e0 % HEADS) == e1 // HEAD_DIM)).astype(BF16)
-    expand2 = ((e0 < 8) & ((e0 % HEADS) == e1 // HEAD_DIM)).astype(BF16)
     lane64 = iota((MID_ROWS, STATS), 1)
 
     def mid_pass(p):
@@ -446,15 +446,31 @@
 
         lax.fori_loop(0, passes, mid_step, 0)
 
-    v["parts"][...] = dot(v["back"][...], v["xs"][...]).astype(BF16)
+    lane128, row128 = iota((128, STATS), 1), iota((128, STATS), 0)
+    to_place = ((row128 < 12) & (row128 % HEADS == lane128 // ROWS)).astype(BF16)
+    diagonal = lane128 % ROWS == row128 % ROWS
+    row8 = iota((8, WIDTH), 0)
     a_copies = []
-    for d in range(1, NREQ):
-        peer = req_peer(d)
-        rows = pl.ds(pl.multiple_of(peer * ROWS, ROWS), ROWS)
-        a_copies.append(
-            send(v["parts"].at[rows], v["arrived"].at[d], asem, d, {"req": peer})
-        )
-    v["arrived"][0] = v["parts"][own_rows, :]
+    for g in range(4):
+        natural = dot(v["back"][g * 128 : (g + 1) * 128, :], v["xs"][...])
+        placed = dot(natural[:, WIDTH:].astype(BF16), to_place)
+        placed = jnp.where(diagonal, placed, 0.0)
+        for d in range(g * 4, g * 4 + 4):
+            rows = slice((d - g * 4) * ROWS, (d - g * 4 + 1) * ROWS)
+            v["parts"][d, :ROWS, :] = natural[rows, :WIDTH].astype(BF16)
+            lse = total(placed[rows], 0)
+            a, b, c = three_terms(jnp.concatenate([lse, jnp.zeros((1, STATS), F32)], axis=1))
+            tail = jnp.where(
+                row8 == 0,
+                a.astype(F32),
+                jnp.where(row8 == 1, b.astype(F32), jnp.where(row8 == 2, c.astype(F32), 0.0)),
+            )
+            v["parts"][d, ROWS:, :] = tail.astype(BF16)
+            if d > 0:
+                a_copies.append(
+                    send(v["parts"].at[d], v["arrived"].at[d], asem, d, {"req": req_peer(d)})
+                )
+    v["arrived"][0] = v["parts"][0]
 
     repeat = (iota((256, ROWS), 0) // 8 == iota((256, ROWS), 1)).astype(BF16)
     head_mask = (r2 % 8) == (c2 // HEAD_DIM)
@@ -482,13 +498,12 @@
     acc = jnp.where(head_mask, acc / row_sum, 0.0)
     leaf_out = jnp.sum(acc.reshape(ROWS, 8, WIDTH), axis=1)
     lse = best + jnp.log(row_sum)
-    spread = jnp.where((r2 % 8)[:, :STATS] == c2[:, :STATS], lse, 0.0)
-    leaf_lse = jnp.sum(spread.reshape(ROWS, 8, STATS), axis=1)
-
-    lane = iota((ROWS, STATS), 1)
+    place = ((r2 % 8) * ROWS + r2 // 8)[:, :STATS] == c2[:, :STATS]
+    leaf_lse = total(jnp.where(place, lse, 0.0), 0)
+
     for copy in a_copies:
         copy.wait_recv()
-    lses = [unpacked_lse(v["arrived"][s, :, WIDTH:].astype(F32)) for s in range(NREQ)]
+    lses = [total(v["arrived"][s, ROWS:, :STATS].astype(F32), 0) for s in range(NREQ)]
     lses.append(leaf_lse)
     best = lses[0]
     for value in lses[1:]:
@@ -497,16 +512,18 @@
     row_sum = shares[0]
     for value in shares[1:]:
         row_sum = row_sum + value
+    diagonal = iota((ROWS, STATS), 1) % ROWS == iota((ROWS, STATS), 0)
+    expand = ((r2 % STATS) // ROWS == c2 // HEAD_DIM).astype(BF16)
+    pieces = []
+    for share in shares:
+        share = jnp.where(diagonal, share / row_sum, 0.0)
+        high = share.astype(BF16)
+        pieces.append(jnp.concatenate([high, (share - high.astype(F32)).astype(BF16)], axis=1))
+    factors = dot(jnp.concatenate(pieces, axis=0), expand)
     attended = jnp.zeros((ROWS, WIDTH), F32)
     for s in range(NREQ + 1):
-        share = shares[s] / row_sum
-        high = share.astype(BF16).astype(F32)
-        both = jnp.where(
-            lane < 4, high, jnp.where(lane < 8, pltpu.roll(share - high, 4, 1), 0.0)
-        )
-        factor = dot(both.astype(BF16), expand2)
-        source = v["arrived"][s, :, :WIDTH].astype(F32) if s < NREQ else leaf_out
-        attended = attended + factor * source
+        source = v["arrived"][s, :ROWS, :].astype(F32) if s < NREQ else leaf_out
+        attended = attended + factors[s * ROWS : (s + 1) * ROWS] * source
     attended = attended.astype(BF16)
 
     own_cols = pl.ds(pl.multiple_of(tp * WIDTH, WIDTH), WIDTH)

time: 48.1 us -> 47.5 us (0.988)
  Pallas kernels: 44.7 us -> 44.1 us
    pallas_call x1, Pallas kernels: 44.7 us -> 44.1 us  [layer_device(): pl.pallas_call(functools.partial(layer_kernel, passes), name='layer' if p...]
where the time goes in v4:
time: 47.5 us; the launch traced here: 47.3 us
  Pallas kernels  44.1 us (93%)
  other arithmetic  1.44 us (3%)
  between operations  0.66 us (1%)
  local copies, waits for them, and re-layouts  0.61 us (1%)
  loops' own time  0.54 us (1%)
    pallas_call x1, Pallas kernels, layer_device(): pl.pallas_call(functools.partial(layer_kernel, passes), name='layer' if p...  44.1 us

profile of v4, /device:TPU:1, one launch (start us, length us, event | category | flops | bytes accessed | tf_op | source)
XLA Modules:
  0.0 47.3 jit_solution(15626364674034212686)
XLA Ops:
  0.0 0.8 %convert_reduce_fusion = s32[16]{0:T(128)S(1)} fusion(s32[512]{0:T(512)} %param.39), kind=kLoop, calls=%fused_computation | loop fusion | flops 24560 | bytes 2112 | tf_op jit(solution)/shard_map/reduce_sum | solution.py:660
  0.8 0.6 %reduce_max.9 = s32[]{:T(128)} reduce(s32[16]{0:T(128)S(1)} %convert_reduce_fusion, s32[]{:T(128)} %constant.2.clone.1), dimensions={0}, to_apply=%region_1.0 | reduce | flops 15 | bytes 72 | tf_op jit(solution)/shard_map/reduce_max | solution.py:665
  2.1 44.6 %conditional.1 = (bf16[32,256]{1,0:T(8,128)(2,1)S(1)}) conditional(s32[]{:T(128)} %convert_element_type.7, (bf16[32,2048]{1,0:T(8,128)(2,1)}, bf16[2048]{0:T(1024)(128)(2,1)}, bf16[2048]{0:T(1024)(128)(2,1)}, s32[512]{0:T(512)}, s32[16]{0:T(128)}, /*index=5*/s32[8]{0:T(128)}, s32[16]{0:T(128)}, s32[32]{0:T(128)}, s32[1,256]{1,0:T(1,128)}, ...), branch_computations={%region_2.0_spmd, %region_3.0_spmd} | conditional | bytes 8 | solution.py:665
  2.3 44.1 %layer.1 = bf16[32,256]{1,0:T(8,128)(2,1)S(1)} custom-call(bf16[32,2048]{1,0:T(8,128)(2,1)} %get-tuple-element.103.refs_0_, bf16[2048]{0:T(1024)(128)(2,1)} %get-tuple-element.104.refs_1_, bf16[2048]{0:T(1024)(128)(2,1)} %get-tuple-element.105.refs_2_, s32[512]{0:T(512)} %get-tuple-element.106.refs_3_, s32[16]{0:T(128)} %get-tuple-element.107.refs_4_, ...), custom_call_target="tpu_custom_call" | custom-call | tf_op jit(solution)/shard_map/cond/branch_1_fun/layer/pallas_call | solution.py:614
  46.7 0.6 %copy.26 = bf16[32,256]{1,0:T(8,128)(2,1)} copy(bf16[32,256]{1,0:T(8,128)(2,1)S(1)} %get-tuple-element.122) | data formatting | bytes 32768

commit v5 on v4

--- a/solution.py
+++ b/solution.py
@@ -25,6 +25,9 @@
 BLOCK = 32
 BLOCKS = 24
 GROUP = 8
+FAR_TP = (4, 3, 5, 2, 6, 1, 7)
+NEAR_TP = FAR_TP[::-1]
+FAR_REQ = (10, 6, 9, 11, 14, 2, 8, 5, 7, 13, 15, 4, 12, 1, 3)
 SORTED = BLOCKS * BLOCK
 MID_ROWS = 64
 STATS = 128
@@ -267,9 +270,9 @@
     own_rows = pl.ds(pl.multiple_of(rank * ROWS, ROWS), ROWS)
     v["qall"][own_rows, :] = queries
     q_slot = v["qall"].at[own_rows]
-    q_copies = [send(q_slot, q_slot, qsem, d, {"req": req_peer(d)}) for d in range(1, NREQ)]
-    for copy in (leaf_copy, wout_copy, wgu_copy, wdn_copy):
-        copy.start()
+    q_copies = [send(q_slot, q_slot, qsem, d, {"req": req_peer(d)}) for d in FAR_REQ]
+    leaf_copy.start()
+    wout_copy.start()
 
     root_row = total(jnp.where(belongs, mp_col, 0.0), 0)
     by_root = (iota((8, 512), 0).astype(F32) == root_row).astype(F32)
@@ -451,7 +454,7 @@
     diagonal = lane128 % ROWS == row128 % ROWS
     row8 = iota((8, WIDTH), 0)
     a_copies = []
-    for g in range(4):
+    for g in (2, 1, 3, 0):
         natural = dot(v["back"][g * 128 : (g + 1) * 128, :], v["xs"][...])
         placed = dot(natural[:, WIDTH:].astype(BF16), to_place)
         placed = jnp.where(diagonal, placed, 0.0)
@@ -470,6 +473,8 @@
                 a_copies.append(
                     send(v["parts"].at[d], v["arrived"].at[d], asem, d, {"req": req_peer(d)})
                 )
+    wgu_copy.start()
+    wdn_copy.start()
     v["arrived"][0] = v["parts"][0]
 
     repeat = (iota((256, ROWS), 0) // 8 == iota((256, ROWS), 1)).astype(BF16)
@@ -529,12 +534,12 @@
     own_cols = pl.ds(pl.multiple_of(tp * WIDTH, WIDTH), WIDTH)
 
     def scatter(left, weight_v, outgoing, incoming, sems):
-        copies = []
-        for d in range(1, NTP):
+        copies = {}
+        for d in FAR_TP:
             peer = tp_peer(d)
             cols = pl.ds(pl.multiple_of(peer * WIDTH, WIDTH), WIDTH)
             outgoing[d] = dot(left, weight_v[:, cols]).astype(BF16)
-            copies.append(send(outgoing.at[d], incoming.at[d], sems, d, {"tp": peer}))
+            copies[d] = send(outgoing.at[d], incoming.at[d], sems, d, {"tp": peer})
         return copies, dot(left, weight_v[:, own_cols])
 
     wout_copy.wait()
@@ -545,19 +550,19 @@
     to_odd = (j2 == 2 * i2 + 1).astype(BF16)
     gain_row = mgain_v[...].reshape(1, D).astype(F32)
     v["gain"][...] = gain_row
-    for d in range(1, NTP):
-        r_copies[d - 1].wait_recv()
+    for d in NEAR_TP:
+        r_copies[d].wait_recv()
         residual = residual + v["rs_in"][d].astype(F32)
 
     v["ag"][0] = residual.astype(BF16)
-    g_copies = [
-        send(v["ag"].at[0], v["ag"].at[d], gsem, d, {"tp": tp_peer(d)}) for d in range(1, NTP)
-    ]
+    g_copies = {
+        d: send(v["ag"].at[0], v["ag"].at[d], gsem, d, {"tp": tp_peer(d)}) for d in FAR_TP
+    }
     wgu_copy.wait()
     squares = jnp.zeros((ROWS, WIDTH), F32)
-    for d in range(NTP):
+    for d in (0, *NEAR_TP):
         if d > 0:
-            g_copies[d - 1].wait_recv()
+            g_copies[d].wait_recv()
         owner = tp_peer(NTP - d)
         part = v["ag"][d].astype(F32)
         squares = squares + part * part
@@ -579,11 +584,12 @@
     wdn_copy.wait()
     d_copies, own_part = scatter(hidden, v["wdn"], v["ds_out"], v["ds_in"], dsem)
     result = residual + own_part
-    for d in range(1, NTP):
-        d_copies[d - 1].wait_recv()
+    for d in NEAR_TP:
+        d_copies[d].wait_recv()
         result = result + v["ds_in"][d].astype(F32)
     out_ref[...] = result.astype(BF16)
-    for copy in held_copies + q_copies + a_copies + r_copies + g_copies + d_copies:
+    late = [*r_copies.values(), *g_copies.values(), *d_copies.values()]
+    for copy in held_copies + q_copies + a_copies + late:
         copy.wait_send()
 
 

time: 47.5 us -> 48.4 us (1.019)
  Pallas kernels: 44.1 us -> 45.1 us
    pallas_call x1, Pallas kernels: 44.1 us -> 45.1 us  [layer_device(): pl.pallas_call(functools.partial(layer_kernel, passes), name='layer' if p...]
where the time goes in v5:
time: 48.4 us; the launch traced here: 48.3 us
  Pallas kernels  45.1 us (93%)
  other arithmetic  1.44 us (3%)
  between operations  0.66 us (1%)
  local copies, waits for them, and re-layouts  0.61 us (1%)
  loops' own time  0.54 us (1%)
    pallas_call x1, Pallas kernels, layer_device(): pl.pallas_call(functools.partial(layer_kernel, passes), name='layer' if p...  45.1 us

profile of v5, /device:TPU:1, one launch (start us, length us, event | category | flops | bytes accessed | tf_op | source)
XLA Modules:
  0.0 48.3 jit_solution(6215154363347105344)
XLA Ops:
  0.0 0.8 %convert_reduce_fusion = s32[16]{0:T(128)S(1)} fusion(s32[512]{0:T(512)} %param.39), kind=kLoop, calls=%fused_computation | loop fusion | flops 24560 | bytes 2112 | tf_op jit(solution)/shard_map/reduce_sum | solution.py:666
  0.8 0.6 %reduce_max.9 = s32[]{:T(128)} reduce(s32[16]{0:T(128)S(1)} %convert_reduce_fusion, s32[]{:T(128)} %constant.2.clone.1), dimensions={0}, to_apply=%region_1.0 | reduce | flops 15 | bytes 72 | tf_op jit(solution)/shard_map/reduce_max | solution.py:671
  2.1 45.6 %conditional.1 = (bf16[32,256]{1,0:T(8,128)(2,1)S(1)}) conditional(s32[]{:T(128)} %convert_element_type.7, (bf16[32,2048]{1,0:T(8,128)(2,1)}, bf16[2048]{0:T(1024)(128)(2,1)}, bf16[2048]{0:T(1024)(128)(2,1)}, s32[512]{0:T(512)}, s32[16]{0:T(128)}, /*index=5*/s32[8]{0:T(128)}, s32[16]{0:T(128)}, s32[32]{0:T(128)}, s32[1,256]{1,0:T(1,128)}, ...), branch_computations={%region_2.0_spmd, %region_3.0_spmd} | conditional | bytes 8 | solution.py:671
  2.3 45.1 %layer.1 = bf16[32,256]{1,0:T(8,128)(2,1)S(1)} custom-call(bf16[32,2048]{1,0:T(8,128)(2,1)} %get-tuple-element.103.refs_0_, bf16[2048]{0:T(1024)(128)(2,1)} %get-tuple-element.104.refs_1_, bf16[2048]{0:T(1024)(128)(2,1)} %get-tuple-element.105.refs_2_, s32[512]{0:T(512)} %get-tuple-element.106.refs_3_, s32[16]{0:T(128)} %get-tuple-element.107.refs_4_, ...), custom_call_target="tpu_custom_call" | custom-call | tf_op jit(solution)/shard_map/cond/branch_1_fun/layer/pallas_call | solution.py:620
  47.7 0.6 %copy.26 = bf16[32,256]{1,0:T(8,128)(2,1)} copy(bf16[32,256]{1,0:T(8,128)(2,1)S(1)} %get-tuple-element.122) | data formatting | bytes 32768

commit v6 on v4

--- a/solution.py
+++ b/solution.py
@@ -333,8 +333,6 @@
 
     mid_copy.wait()
     split_pairs(split, v["mid"], v["mid_k"], v["mid_v"], 16)
-    key_new = rope(dot(normed, v["wk"][...]), cosines, sines).astype(BF16)
-    value_new = dot(normed, v["wv"][...]).astype(BF16)
 
     for copy in q_copies:
         copy.wait_recv()
@@ -373,6 +371,15 @@
 
     lax.fori_loop(0, BLOCKS // GROUP, root_blocks, 0)
 
+    mid_mask = (iota((256, WIDTH), 0) // MID_ROWS == iota((256, WIDTH), 1) // HEAD_DIM).astype(BF16)
+    e0, e1 = iota((STATS, WIDTH), 0), iota((STATS, WIDTH), 1)
+    expand3 = ((e0 < 12) & ((e0 % HEADS) == e1 // HEAD_DIM)).astype(BF16)
+    lane64 = iota((MID_ROWS, STATS), 1)
+    lane128, row128 = iota((128, STATS), 1), iota((128, STATS), 0)
+    to_place = ((row128 < 12) & (row128 % HEADS == lane128 // ROWS)).astype(BF16)
+    in_place = lane128 % ROWS == row128 % ROWS
+    row8 = iota((8, WIDTH), 0)
+
     for copy in [held_copies[2]] + held_copies[5:]:
         copy.wait_recv()
     square = jnp.zeros((256, 1), F32)
@@ -389,11 +396,6 @@
         values = values + dot(part, v["wv"][rows, :])
     v["new_k"][...] = rope(keys, held_cos, held_sin).astype(BF16)
     v["new_v"][...] = values.astype(BF16)
-
-    mid_mask = (iota((256, WIDTH), 0) // MID_ROWS == iota((256, WIDTH), 1) // HEAD_DIM).astype(BF16)
-    e0, e1 = iota((STATS, WIDTH), 0), iota((STATS, WIDTH), 1)
-    expand3 = ((e0 < 12) & ((e0 % HEADS) == e1 // HEAD_DIM)).astype(BF16)
-    lane64 = iota((MID_ROWS, STATS), 1)
 
     def mid_pass(p):
         chosen = (iota((MID_ROWS, 512), 0) + p * MID_ROWS == mid_order.astype(I32)) & in_mid
@@ -446,15 +448,11 @@
 
         lax.fori_loop(0, passes, mid_step, 0)
 
-    lane128, row128 = iota((128, STATS), 1), iota((128, STATS), 0)
-    to_place = ((row128 < 12) & (row128 % HEADS == lane128 // ROWS)).astype(BF16)
-    diagonal = lane128 % ROWS == row128 % ROWS
-    row8 = iota((8, WIDTH), 0)
     a_copies = []
     for g in range(4):
         natural = dot(v["back"][g * 128 : (g + 1) * 128, :], v["xs"][...])
         placed = dot(natural[:, WIDTH:].astype(BF16), to_place)
-        placed = jnp.where(diagonal, placed, 0.0)
+        placed = jnp.where(in_place, placed, 0.0)
         for d in range(g * 4, g * 4 + 4):
             rows = slice((d - g * 4) * ROWS, (d - g * 4 + 1) * ROWS)
             v["parts"][d, :ROWS, :] = natural[rows, :WIDTH].astype(BF16)
@@ -472,6 +470,8 @@
                 )
     v["arrived"][0] = v["parts"][0]
 
+    key_new = rope(dot(normed, v["wk"][...]), cosines, sines).astype(BF16)
+    value_new = dot(normed, v["wv"][...]).astype(BF16)
     repeat = (iota((256, ROWS), 0) // 8 == iota((256, ROWS), 1)).astype(BF16)
     head_mask = (r2 % 8) == (c2 // HEAD_DIM)
     qrep = jnp.where(head_mask, dot(repeat, queries), 0.0)
@@ -501,6 +501,8 @@
     place = ((r2 % 8) * ROWS + r2 // 8)[:, :STATS] == c2[:, :STATS]
     leaf_lse = total(jnp.where(place, lse, 0.0), 0)
 
+    diagonal = iota((ROWS, STATS), 1) % ROWS == iota((ROWS, STATS), 0)
+    expand = ((r2 % STATS) // ROWS == c2 // HEAD_DIM).astype(BF16)
     for copy in a_copies:
         copy.wait_recv()
     lses = [total(v["arrived"][s, ROWS:, :STATS].astype(F32), 0) for s in range(NREQ)]
@@ -512,8 +514,6 @@
     row_sum = shares[0]
     for value in shares[1:]:
         row_sum = row_sum + value
-    diagonal = iota((ROWS, STATS), 1) % ROWS == iota((ROWS, STATS), 0)
-    expand = ((r2 % STATS) // ROWS == c2 // HEAD_DIM).astype(BF16)
     pieces = []
     for share in shares:
         share = jnp.where(diagonal, share / row_sum, 0.0)

time: 47.5 us -> 47.5 us (level)
  no operation moved by 1% of the time
where the time goes in v6:
time: 47.5 us; the launch traced here: 47.3 us
  Pallas kernels  44.1 us (93%)
  other arithmetic  1.44 us (3%)
  between operations  0.66 us (1%)
  local copies, waits for them, and re-layouts  0.61 us (1%)
  loops' own time  0.54 us (1%)
    pallas_call x1, Pallas kernels, layer_device(): pl.pallas_call(functools.partial(layer_kernel, passes), name='layer' if p...  44.1 us

profile of v6, /device:TPU:1, one launch (start us, length us, event | category | flops | bytes accessed | tf_op | source)
XLA Modules:
  0.0 47.3 jit_solution(2359677752053683090)
XLA Ops:
  0.0 0.8 %convert_reduce_fusion = s32[16]{0:T(128)S(1)} fusion(s32[512]{0:T(512)} %param.39), kind=kLoop, calls=%fused_computation | loop fusion | flops 24560 | bytes 2112 | tf_op jit(solution)/shard_map/reduce_sum | solution.py:660
  0.8 0.6 %reduce_max.9 = s32[]{:T(128)} reduce(s32[16]{0:T(128)S(1)} %convert_reduce_fusion, s32[]{:T(128)} %constant.2.clone.1), dimensions={0}, to_apply=%region_1.0 | reduce | flops 15 | bytes 72 | tf_op jit(solution)/shard_map/reduce_max | solution.py:665
  2.1 44.6 %conditional.1 = (bf16[32,256]{1,0:T(8,128)(2,1)S(1)}) conditional(s32[]{:T(128)} %convert_element_type.7, (bf16[32,2048]{1,0:T(8,128)(2,1)}, bf16[2048]{0:T(1024)(128)(2,1)}, bf16[2048]{0:T(1024)(128)(2,1)}, s32[512]{0:T(512)}, s32[16]{0:T(128)}, /*index=5*/s32[8]{0:T(128)}, s32[16]{0:T(128)}, s32[32]{0:T(128)}, s32[1,256]{1,0:T(1,128)}, ...), branch_computations={%region_2.0_spmd, %region_3.0_spmd} | conditional | bytes 8 | solution.py:665
  2.3 44.1 %layer.1 = bf16[32,256]{1,0:T(8,128)(2,1)S(1)} custom-call(bf16[32,2048]{1,0:T(8,128)(2,1)} %get-tuple-element.103.refs_0_, bf16[2048]{0:T(1024)(128)(2,1)} %get-tuple-element.104.refs_1_, bf16[2048]{0:T(1024)(128)(2,1)} %get-tuple-element.105.refs_2_, s32[512]{0:T(512)} %get-tuple-element.106.refs_3_, s32[16]{0:T(128)} %get-tuple-element.107.refs_4_, ...), custom_call_target="tpu_custom_call" | custom-call | tf_op jit(solution)/shard_map/cond/branch_1_fun/layer/pallas_call | solution.py:614
  46.7 0.6 %copy.26 = bf16[32,256]{1,0:T(8,128)(2,1)} copy(bf16[32,256]{1,0:T(8,128)(2,1)S(1)} %get-tuple-element.122) | data formatting | bytes 32768
